TPU v7x, 32 devices: a whole 2x2x4 slice. The times are simulated.
32 devices in a mesh: rows: 16 (over z, y, core), cols: 2 (over x).
Axes of the slice: x: 2, y: 2, z: 4, core: 2. Of those that a mesh axis runs over, the one named last changes fastest.
Arguments:
- features: bfloat16 [4096, 128], P('rows', 'cols'), may hold values from -6 to 6
- adj_tiles: bfloat16 [1536, 128, 128], P('rows'), may hold values from -0.109375 to 0.109375
- tile_src: int32 [1536], P('rows'), may hold values from 0 to 31, as said below
- tile_dst: int32 [1536], P('rows'), may hold values from 0 to 1, as said below
- tile_count: int32 [16], P('rows'), may hold values from 24 to 96, as said below
- cluster_size: int32 [32], P('rows'), may hold values from 64 to 128, as said below
- weight: bfloat16 [128, 256], P(None, 'cols'), may hold values from -0.5 to 0.5
- bias: float32 [256], P('cols'), may hold values from -3 to 3
- grad_out: bfloat16 [4096, 256], P('rows', 'cols'), may hold values from -6 to 6
Outputs:
- hidden: bfloat16 [4096, 256], P('rows', 'cols')
- grad_weight: float32 [128, 256], P(None, 'cols')
- grad_bias: float32 [256], P('cols')
- grad_features: bfloat16 [4096, 128], P('rows', 'cols')
Inputs may be any that keep to these rules, and one draw needn't show every extreme that they name: In row group r, slots 0 to tile_count[r] - 1 of its 96 slots hold tiles, in non-decreasing order of tile_src; the later slots are unused: their tile_src and tile_dst hold 0, and their adj_tiles hold arbitrary values that must not contribute. A used slot's column cluster belongs to row group r itself or to a row group whose index differs from r in exactly one bit (row group g holds clusters g * 2 to g * 2 + 1). Equal (row, column) pairs may repeat and then add. `tile_dst`: unused slots hold 0. `tile_count`: some row groups use all 96 slots. `cluster_size`: the real nodes of a cluster are its first ones; some cluster is full.
All inputs are finite; a program needn't handle non-finite values.
Results may differ from a plain program's by a relative error of at most 0.006.
Values may be sent and summed in bfloat16 or wider, within the bound.
No kernel may reach another device: no remote copies, remote signals or barrier semaphores. Data moves between devices by JAX's collectives and lax.ppermute only.
A program may use at most 64 MiB of HBM per device.

v0:
```python
import functools
import math

import jax
import jax.numpy as jnp
from jax import lax
from jax.experimental import pallas as pl
from jax.experimental.pallas import tpu as pltpu
from jax.sharding import PartitionSpec as P


TILE_GROUP = 16
F32, BF16 = jnp.float32, jnp.bfloat16
VMEM = pl.BlockSpec(memory_space=pltpu.VMEM)
FAR = pl.BlockSpec(memory_space=pltpu.VMEM)
SMEM = pl.BlockSpec(memory_space=pltpu.SMEM)
HBM = pl.BlockSpec(memory_space=pl.ANY)


def partner(shard, axis, bit):
    return lax.ppermute(shard, axis, [(i, i ^ 1 << bit) for i in range(lax.axis_size(axis))])


def near(array):
    return pltpu.with_memory_space_constraint(array, pltpu.VMEM)


def kernel_call(kernel, out_shape, in_specs, args, out_specs=None, scratch=()):
    args = [near(arg) if spec is VMEM else arg for spec, arg in zip(in_specs, args, strict=True)]
    outs = jax.tree.map(lambda _: VMEM, out_shape, is_leaf=lambda x: hasattr(x, "shape"))
    return pl.pallas_call(
        kernel,
        out_shape=out_shape,
        in_specs=in_specs,
        out_specs=outs if out_specs is None else out_specs,
        scratch_shapes=list(scratch),
    )(*args)


def near_out(shape, dtype):
    return pltpu.VMEM(shape, dtype)


def dot(a, b, contract=(1, 0)):
    return lax.dot_general(
        a, b, (((contract[0],), (contract[1],)), ((), ())), preferred_element_type=F32
    )


def live_rows(sizes, clusters, width):
    node = lax.broadcasted_iota(jnp.int32, (width, 1), 0)
    return jnp.concatenate([(node < sizes[c]).astype(F32) for c in range(clusters)], axis=0)


def build_kernel(levels, clusters, tiles, src, dst, count, gout, weight, bias, hi, lo, pack, acc, held, sems, side):
    slots, width = tiles.shape[0], tiles.shape[1]
    rows, hidden = gout.shape
    feats = weight.shape[0]
    used = count[0]
    me = lax.axis_index("rows")
    starts = list(range(0, slots, TILE_GROUP))

    def fetch(first):
        size = min(TILE_GROUP, slots - first)
        return pltpu.make_async_copy(
            tiles.at[pl.ds(first, size)], held.at[pl.ds(first, size)], sems.at[first // TILE_GROUP]
        )

    for first in starts:
        @pl.when(first < used)
        def _(first=first):
            fetch(first).start()
    sides = (
        pltpu.make_async_copy(gout, pack.at[pl.ds(0, rows)], side.at[0]),
        pltpu.make_async_copy(weight, pack.at[pl.ds(rows, feats)], side.at[1]),
    )
    for copy in sides:
        copy.start()
    value = bias[...]
    top = value.astype(BF16).astype(F32)
    rest = value - top
    middle = rest.astype(BF16).astype(F32)
    row = lax.broadcasted_iota(jnp.int32, (16, hidden), 0)
    parts = jnp.where(row == 0, top, jnp.where(row == 1, middle, jnp.where(row == 2, rest - middle, 0.0)))
    pack[pl.ds(rows + feats, 16), :] = parts.astype(BF16)
    acc[...] = jnp.zeros_like(acc)

    def add(slot, carry):
        source = src[slot]
        group = lax.div(source, clusters)
        differs = jnp.bitwise_xor(group, me)
        column = source - group * clusters
        for bit in range(levels):
            column = column + jnp.where(differs == 1 << bit, (bit + 1) * clusters, 0)
        at = (
            pl.ds(pl.multiple_of(dst[slot] * width, width), width),
            pl.ds(pl.multiple_of(column * width, width), width),
        )
        acc[at] = acc[at] + held[slot].astype(F32)
        return carry

    for first in starts:
        @pl.when(first < used)
        def _(first=first):
            fetch(first).wait()
            lax.fori_loop(first, jnp.minimum(first + TILE_GROUP, used), add, 0)

    total = acc[...]
    high = total.astype(BF16)
    hi[...] = high
    lo[...] = (total - high.astype(F32)).astype(BF16)
    for copy in sides:
        copy.wait()


def merge_kernel(clusters, own, other, sizes, out):
    mine, theirs = own[...].astype(F32), other[...].astype(F32)
    first = lax.axis_index("cols") == 0
    both = jnp.concatenate(
        [jnp.where(first, mine, theirs), jnp.where(first, theirs, mine)], axis=0
    )
    live = live_rows(sizes, clusters, own.shape[1] // clusters)
    out[...] = (both.T * live).astype(BF16)


def main_kernel(levels, clusters, *refs):
    hi, lo, gout, weight, bias, pack, sizes = refs[:7]
    tables = refs[7 : 8 + levels]
    hidden_out, sums, grad_out_t, hidden_near, sem = refs[8 + levels :]
    nodes, feats = tables[0].shape
    half = grad_out_t.shape[0]
    agg = jnp.zeros((nodes, feats), F32)
    for level, table in enumerate(tables):
        value = table[...]
        at = (slice(None), pl.ds(level * nodes, nodes))
        agg = agg + dot(hi[at], value) + dot(lo[at], value)
    agg = agg.astype(BF16)
    live = live_rows(sizes, clusters, nodes // clusters)
    mine = pl.ds(pl.multiple_of(lax.axis_index("cols") * half, half), half)

    def dense(matrix, shift, cotangent):
        pre = dot(agg, matrix) + shift
        sig = jax.nn.sigmoid(pre)
        grad = cotangent.astype(F32) * sig * (1.0 + pre * (1.0 - sig)) * live
        return pre * sig * live, grad.astype(BF16)

    hidden, grad_pre = dense(weight[...], bias[...], gout[...])
    hidden_near[...] = hidden.astype(BF16)
    leave = pltpu.make_async_copy(hidden_near, hidden_out, sem)
    leave.start()
    sums[pl.ds(0, feats), :] = dot(agg, grad_pre, (0, 0))
    column_sums = jnp.sum(grad_pre.astype(F32), axis=0, keepdims=True)
    sums[pl.ds(feats, 8), :] = jnp.broadcast_to(column_sums, (8, column_sums.shape[1]))
    shift = pack[pl.ds(nodes + feats, 16), :].astype(F32)
    shift = shift[0:1] + shift[1:2] + shift[2:3]
    _, grad_other = dense(pack[pl.ds(nodes, feats), :], shift, pack[pl.ds(0, nodes), :])
    other_rows = pl.ds(pl.multiple_of(nodes + lax.axis_index("cols") * half, half), half)
    grad_agg = dot(weight[mine, :], grad_pre, (1, 1)) + dot(pack[other_rows, :], grad_other, (1, 1))
    grad_out_t[...] = grad_agg.astype(BF16)
    leave.wait()


def spread_kernel(levels, hi, lo, grad_t, *outs):
    value = grad_t[...]
    nodes = value.shape[1]
    for level in range(levels + 1):
        at = (slice(None), pl.ds(level * nodes, nodes))
        outs[level][...] = dot(value, hi[at]) + dot(value, lo[at])


def finish_kernel(clusters, *refs):
    sizes, out = refs[0], refs[-1]
    total = refs[1][...]
    for part in refs[2:-1]:
        total = total + part[...]
    width = total.shape[1] // clusters
    node = lax.broadcasted_iota(jnp.int32, (1, width), 1)
    live = jnp.concatenate([(node < sizes[c]).astype(F32) for c in range(clusters)], axis=1)
    out[...] = (total * live).astype(BF16)


def add_kernel(own, other, out):
    out[...] = own[...] + other[...]


def add(own, other):
    return kernel_call(add_kernel, near_out(own.shape, own.dtype), [VMEM, VMEM], (own, other))


def scale_kernel(scale, own, other, grad_weight, grad_bias):
    feats = grad_weight.shape[0]
    grad_weight[...] = (own[pl.ds(0, feats), :] + other[pl.ds(0, feats), :]) * scale
    grad_bias[...] = (own[pl.ds(feats, 1), :] + other[pl.ds(feats, 1), :]) * scale


def local(features, adj_tiles, tile_src, tile_dst, tile_count, cluster_size, weight, bias, grad_out):
    clusters = cluster_size.shape[0]
    slots, width = adj_tiles.shape[:2]
    nodes, half = features.shape
    feats, hidden = weight.shape
    levels = lax.axis_size("rows").bit_length() - 1
    columns = (levels + 1) * nodes
    bias = bias.reshape(1, hidden)
    own = near(features.T)
    other = partner(own, "cols", 0)
    hi, lo, pack = kernel_call(
        functools.partial(build_kernel, levels, clusters),
        (
            near_out((nodes, columns), BF16),
            near_out((nodes, columns), BF16),
            near_out((nodes + feats + 16, hidden), BF16),
        ),
        [HBM, SMEM, SMEM, SMEM, HBM, HBM, FAR],
        (adj_tiles, tile_src, tile_dst, tile_count, grad_out, weight, bias),
        scratch=[
            pltpu.VMEM((nodes, columns), F32),
            pltpu.VMEM((slots, width, width), BF16),
            pltpu.SemaphoreType.DMA((-(-slots // TILE_GROUP),)),
            pltpu.SemaphoreType.DMA((2,)),
        ],
    )
    table = kernel_call(
        functools.partial(merge_kernel, clusters),
        near_out((nodes, feats), BF16),
        [VMEM, VMEM, SMEM],
        (own, other, cluster_size),
    )
    tables = [table]
    for bit in range(levels):
        tables.append(partner(table, "rows", bit))
    pack = partner(pack, "cols", 0)
    hidden_out, sums, grad_agg = kernel_call(
        functools.partial(main_kernel, levels, clusters),
        (
            jax.ShapeDtypeStruct((nodes, hidden), BF16),
            near_out((feats + 8, hidden), F32),
            near_out((half, nodes), BF16),
        ),
        [VMEM] * 5 + [VMEM, SMEM] + [VMEM] * (levels + 1),
        (hi, lo, grad_out, weight, bias, pack, cluster_size, *tables),
        out_specs=(HBM, VMEM, VMEM),
        scratch=[pltpu.VMEM((nodes, hidden), BF16), pltpu.SemaphoreType.DMA],
    )
    parts = kernel_call(
        functools.partial(spread_kernel, levels),
        [near_out((half, nodes), F32)] * (levels + 1),
        [VMEM] * 3,
        (hi, lo, grad_agg),
    )
    received = []
    for bit in range(levels):
        received.append(partner(parts[bit + 1], "rows", bit))
    moved = None
    for bit in range(levels):
        sums = add(sums, moved) if bit else sums
        moved = partner(sums, "rows", bit)
    grad_features = kernel_call(
        functools.partial(finish_kernel, clusters),
        jax.ShapeDtypeStruct((half, nodes), BF16),
        [SMEM] + [VMEM] * (levels + 1),
        (cluster_size, parts[0], *received),
    )
    grad_scale = 1.0 / math.sqrt(nodes * lax.axis_size("rows"))
    grad_weight, grad_bias = kernel_call(
        functools.partial(scale_kernel, grad_scale),
        (jax.ShapeDtypeStruct((feats, hidden), F32), jax.ShapeDtypeStruct((1, hidden), F32)),
        [VMEM, VMEM],
        (sums, moved),
    )
    return (hidden_out, grad_weight, grad_bias.reshape(hidden), grad_features.T)


def solution(mesh):
    return jax.shard_map(
        local,
        mesh=mesh,
        in_specs=(
            P("rows", "cols"),
            P("rows", None, None),
            P("rows"),
            P("rows"),
            P("rows"),
            P("rows"),
            P(None, "cols"),
            P("cols"),
            P("rows", "cols"),
        ),
        out_specs=(P("rows", "cols"), P(None, "cols"), P("cols"), P("rows", "cols")),
        check_vma=False,
    )
```

profile of v0, /device:TPU:0, one launch (start us, length us, event | category | flops | bytes accessed | tf_op | source)
XLA Modules:
  0.0 44.5 jit_solution(367342057877454621)
XLA Ops:
  1.4 2.6 %shard_map.120 = (bf16[256,1280]{1,0:T(8,128)(2,1)S(1)}, bf16[256,1280]{1,0:T(8,128)(2,1)S(1)}, bf16[400,128]{1,0:T(8,128)(2,1)S(1)}) custom-call(bf16[96,128,128]{2,1,0:T(8,128)(2,1)} %tiles.1, s32[96]{0:T(128)} %src.1, s32[96]{0:T(128)} %dst.1, s32[1]{0:T(128)S(6)} %copy.13.count, bf16[256,128]{1,0:T(8,128)(2,1)} %refs_2_.1, bf16[128,128]{1,0:T(8,128)(2,1)} %refs_3_.1, ...), custom_call_target="tpu_custom_call" | custom-call | tf_op jit(solution)/shard_map/pallas_call | solution.py:31
  3.9 3.0 %collective-permute-start = (bf16[400,128]{1,0:T(8,128)(2,1)S(1)}, bf16[400,128]{1,0:T(8,128)(2,1)S(1)}, u32[]{:S(2)}, u32[]{:S(2)}) collective-permute-start(bf16[400,128]{1,0:T(8,128)(2,1)S(1)} %get-tuple-element.19), channel_id=1, source_target_pairs={{0,1},{1,0},{2,3},{3,2},{4,5},{5,4},{6,7},{7,6},{8,9},{9,8},{10,11... | collective-permute-start | bytes 307208 | tf_op jit(solution)/shard_map/ppermute | solution.py:21
  7.0 3.8 %collective-permute-done.1.other = bf16[64,256]{1,0:T(8,128)(2,1)S(1)} collective-permute-done((bf16[64,256]{1,0:T(8,128)(2,1)S(1)}, bf16[64,256]{1,0:T(8,128)(2,1)S(1)}, u32[]{:S(2)}, u32[]{:S(2)}) %collective-permute-start.1) | collective-permute-done | bytes 32800 | tf_op jit(solution)/shard_map/ppermute | solution.py:21
  10.9 0.8 %shard_map.121.refs_7_ = bf16[256,128]{1,0:T(8,128)(2,1)S(1)} custom-call(bf16[64,256]{1,0:T(8,128)(2,1)S(1)} %bitcast.5, bf16[64,256]{1,0:T(8,128)(2,1)S(1)} %collective-permute-done.1.other, s32[2]{0:T(128)} %refs_0_.1), custom_call_target="tpu_custom_call" | custom-call | tf_op jit(solution)/shard_map/pallas_call | solution.py:31
  11.6 4.0 %collective-permute-start.5 = (bf16[256,128]{1,0:T(8,128)(2,1)S(1)}, bf16[256,128]{1,0:T(8,128)(2,1)S(1)}, u32[]{:S(2)}, u32[]{:S(2)}) collective-permute-start(bf16[256,128]{1,0:T(8,128)(2,1)S(1)} %shard_map.121.refs_7_), channel_id=1, source_target_pairs={{0,16},{2,18},{4,20},{6,22},{8,24},{10,26},{12,28},{14,30},{16,0},... | collective-permute-start | bytes 196616 | tf_op jit(solution)/shard_map/ppermute | solution.py:21
  15.6 0.5 %collective-permute-start.4 = (bf16[256,128]{1,0:T(8,128)(2,1)S(1)}, bf16[256,128]{1,0:T(8,128)(2,1)S(1)}, u32[]{:S(2)}, u32[]{:S(2)}) collective-permute-start(bf16[256,128]{1,0:T(8,128)(2,1)S(1)} %shard_map.121.refs_7_), channel_id=1, source_target_pairs={{0,8},{2,10},{4,12},{6,14},{8,0},{10,2},{12,4},{14,6},{16,24},{18,... | collective-permute-start | bytes 196616 | tf_op jit(solution)/shard_map/ppermute | solution.py:21
  16.1 1.5 %collective-permute-start.3 = (bf16[256,128]{1,0:T(8,128)(2,1)S(1)}, bf16[256,128]{1,0:T(8,128)(2,1)S(1)}, u32[]{:S(2)}, u32[]{:S(2)}) collective-permute-start(bf16[256,128]{1,0:T(8,128)(2,1)S(1)} %shard_map.121.refs_7_), channel_id=1, source_target_pairs={{0,4},{2,6},{4,0},{6,2},{8,12},{10,14},{12,8},{14,10},{16,20},{18,... | collective-permute-start | bytes 196616 | tf_op jit(solution)/shard_map/ppermute | solution.py:21
  17.6 1.0 %collective-permute-done.5.refs_11_ = bf16[256,128]{1,0:T(8,128)(2,1)S(1)} collective-permute-done((bf16[256,128]{1,0:T(8,128)(2,1)S(1)}, bf16[256,128]{1,0:T(8,128)(2,1)S(1)}, u32[]{:S(2)}, u32[]{:S(2)}) %collective-permute-start.5) | collective-permute-done | bytes 65568 | tf_op jit(solution)/shard_map/ppermute | solution.py:21
  18.6 1.3 %collective-permute-done.4.refs_10_ = bf16[256,128]{1,0:T(8,128)(2,1)S(1)} collective-permute-done((bf16[256,128]{1,0:T(8,128)(2,1)S(1)}, bf16[256,128]{1,0:T(8,128)(2,1)S(1)}, u32[]{:S(2)}, u32[]{:S(2)}) %collective-permute-start.4) | collective-permute-done | bytes 65568 | tf_op jit(solution)/shard_map/ppermute | solution.py:21
  19.9 0.5 %collective-permute-done.3.refs_9_ = bf16[256,128]{1,0:T(8,128)(2,1)S(1)} collective-permute-done((bf16[256,128]{1,0:T(8,128)(2,1)S(1)}, bf16[256,128]{1,0:T(8,128)(2,1)S(1)}, u32[]{:S(2)}, u32[]{:S(2)}) %collective-permute-start.3) | collective-permute-done | bytes 65568 | tf_op jit(solution)/shard_map/ppermute | solution.py:21
  20.4 1.9 %shard_map.122 = (bf16[256,128]{1,0:T(8,128)(2,1)}, f32[136,128]{1,0:T(8,128)S(1)}, bf16[64,256]{1,0:T(8,128)(2,1)S(1)}) custom-call(bf16[256,1280]{1,0:T(8,128)(2,1)S(1)} %get-tuple-element.17.refs_0_.hi, bf16[256,1280]{1,0:T(8,128)(2,1)S(1)} %get-tuple-element.18.refs_1_.lo, bf16[256,128]{1,0:T(8,128)(2,1)S(1)} %copy-done, bf16[128,128]{1,0:T(8,128)(2,1)S(1)} %copy-done.1, ...), custom_call_target="tpu_custom_call" | custom-call | tf_op jit(solution)/shard_map/pallas_call | solution.py:31
  22.4 1.2 %collective-permute-done.6.other = f32[136,128]{1,0:T(8,128)S(1)} collective-permute-done((f32[136,128]{1,0:T(8,128)S(1)}, f32[136,128]{1,0:T(8,128)S(1)}, u32[]{:S(2)}, u32[]{:S(2)}) %collective-permute-start.6) | collective-permute-done | bytes 69664 | tf_op jit(solution)/shard_map/ppermute | solution.py:21
  23.7 1.5 %collective-permute-start.7 = (f32[136,128]{1,0:T(8,128)S(1)}, f32[136,128]{1,0:T(8,128)S(1)}, u32[]{:S(2)}, u32[]{:S(2)}) collective-permute-start(f32[136,128]{1,0:T(8,128)S(1)} %shard_map.123.own), channel_id=1, source_target_pairs={{0,4},{2,6},{4,0},{6,2},{8,12},{10,14},{12,8},{14,10},{16,20},{18,... | collective-permute-start | bytes 208904 | tf_op jit(solution)/shard_map/ppermute | solution.py:21
  25.2 2.8 %collective-permute-done.7.other = f32[136,128]{1,0:T(8,128)S(1)} collective-permute-done((f32[136,128]{1,0:T(8,128)S(1)}, f32[136,128]{1,0:T(8,128)S(1)}, u32[]{:S(2)}, u32[]{:S(2)}) %collective-permute-start.7) | collective-permute-done | bytes 69664 | tf_op jit(solution)/shard_map/ppermute | solution.py:21
  28.1 1.6 %collective-permute-start.8 = (f32[136,128]{1,0:T(8,128)S(1)}, f32[136,128]{1,0:T(8,128)S(1)}, u32[]{:S(2)}, u32[]{:S(2)}) collective-permute-start(f32[136,128]{1,0:T(8,128)S(1)} %shard_map.124.own), channel_id=1, source_target_pairs={{0,8},{2,10},{4,12},{6,14},{8,0},{10,2},{12,4},{14,6},{16,24},{18,... | collective-permute-start | bytes 208904 | tf_op jit(solution)/shard_map/ppermute | solution.py:21
  29.7 2.8 %collective-permute-done.8.other = f32[136,128]{1,0:T(8,128)S(1)} collective-permute-done((f32[136,128]{1,0:T(8,128)S(1)}, f32[136,128]{1,0:T(8,128)S(1)}, u32[]{:S(2)}, u32[]{:S(2)}) %collective-permute-start.8) | collective-permute-done | bytes 69664 | tf_op jit(solution)/shard_map/ppermute | solution.py:21
  32.5 0.5 %collective-permute-start.9 = (f32[136,128]{1,0:T(8,128)S(1)}, f32[136,128]{1,0:T(8,128)S(1)}, u32[]{:S(2)}, u32[]{:S(2)}) collective-permute-start(f32[136,128]{1,0:T(8,128)S(1)} %shard_map.125.own), channel_id=1, source_target_pairs={{0,16},{2,18},{4,20},{6,22},{8,24},{10,26},{12,28},{14,30},{16,0},... | collective-permute-start | bytes 208904 | tf_op jit(solution)/shard_map/ppermute | solution.py:21
  33.4 1.5 %collective-permute-start.11 = (f32[64,256]{1,0:T(8,128)S(1)}, f32[64,256]{1,0:T(8,128)S(1)}, u32[]{:S(2)}, u32[]{:S(2)}) collective-permute-start(f32[64,256]{1,0:T(8,128)S(1)} %get-tuple-element.27), channel_id=1, source_target_pairs={{0,4},{2,6},{4,0},{6,2},{8,12},{10,14},{12,8},{14,10},{16,20},{18,... | collective-permute-start | bytes 196616 | tf_op jit(solution)/shard_map/ppermute | solution.py:21
  34.9 1.5 %collective-permute-start.12 = (f32[64,256]{1,0:T(8,128)S(1)}, f32[64,256]{1,0:T(8,128)S(1)}, u32[]{:S(2)}, u32[]{:S(2)}) collective-permute-start(f32[64,256]{1,0:T(8,128)S(1)} %get-tuple-element.28), channel_id=1, source_target_pairs={{0,8},{2,10},{4,12},{6,14},{8,0},{10,2},{12,4},{14,6},{16,24},{18,... | collective-permute-start | bytes 196616 | tf_op jit(solution)/shard_map/ppermute | solution.py:21
  36.3 1.8 %collective-permute-start.13 = (f32[64,256]{1,0:T(8,128)S(1)}, f32[64,256]{1,0:T(8,128)S(1)}, u32[]{:S(2)}, u32[]{:S(2)}) collective-permute-start(f32[64,256]{1,0:T(8,128)S(1)} %get-tuple-element.29), channel_id=1, source_target_pairs={{0,16},{2,18},{4,20},{6,22},{8,24},{10,26},{12,28},{14,30},{16,0},... | collective-permute-start | bytes 196616 | tf_op jit(solution)/shard_map/ppermute | solution.py:21
  38.1 1.0 %collective-permute-done.12.refs_4_ = f32[64,256]{1,0:T(8,128)S(1)} collective-permute-done((f32[64,256]{1,0:T(8,128)S(1)}, f32[64,256]{1,0:T(8,128)S(1)}, u32[]{:S(2)}, u32[]{:S(2)}) %collective-permute-start.12) | collective-permute-done | bytes 65568 | tf_op jit(solution)/shard_map/ppermute | solution.py:21
  39.2 3.4 %collective-permute-done.13.refs_5_ = f32[64,256]{1,0:T(8,128)S(1)} collective-permute-done((f32[64,256]{1,0:T(8,128)S(1)}, f32[64,256]{1,0:T(8,128)S(1)}, u32[]{:S(2)}, u32[]{:S(2)}) %collective-permute-start.13) | collective-permute-done | bytes 65568 | tf_op jit(solution)/shard_map/ppermute | solution.py:21
  42.6 1.3 %shard_map.128 = bf16[64,256]{1,0:T(8,128)(2,1)} custom-call(s32[2]{0:T(128)} %refs_0_.1, f32[64,256]{1,0:T(8,128)S(1)} %get-tuple-element.25.refs_1_, f32[64,256]{1,0:T(8,128)S(1)} %collective-permute-done.10.refs_2_, f32[64,256]{1,0:T(8,128)S(1)} %collective-permute-done.11.refs_3_, f32[64,256]{1,0:T(8,128)S(1)} %collective-permute-done.12.refs_4_, ...), custom_call_target="tpu_custom_call" | custom-call | tf_op jit(solution)/shard_map/pallas_call | solution.py:31
  43.9 0.6 %shard_map.126 = (f32[128,128]{1,0:T(8,128)}, f32[1,128]{1,0:T(1,128)}) custom-call(f32[136,128]{1,0:T(8,128)S(1)} %shard_map.125.own, f32[136,128]{1,0:T(8,128)S(1)} %collective-permute-done.9.other), custom_call_target="tpu_custom_call" | custom-call | tf_op jit(solution)/shard_map/pallas_call | solution.py:31
  (21 shorter events, 0.6 us)
Async XLA Ops:
  0.6 19.8 %copy-start = (bf16[256,128]{1,0:T(8,128)(2,1)S(1)}, bf16[256,128]{1,0:T(8,128)(2,1)}, u32[]{:S(2)}) copy-start(bf16[256,128]{1,0:T(8,128)(2,1)} %refs_2_.1) | copy-start | bytes 196612
  0.6 19.8 %copy-start.1 = (bf16[128,128]{1,0:T(8,128)(2,1)S(1)}, bf16[128,128]{1,0:T(8,128)(2,1)}, u32[]{:S(2)}) copy-start(bf16[128,128]{1,0:T(8,128)(2,1)} %refs_3_.1) | copy-start | bytes 98308
  0.7 19.8 %copy-start.3 = (f32[128]{0:T(128)S(1)}, f32[128]{0:T(128)}, u32[]{:S(2)}) copy-start(f32[128]{0:T(128)} %param.16) | copy-start | bytes 1540
  0.7 6.3 %copy-start.2 = (bf16[256,64]{0,1:T(8,128)(2,1)S(1)}, bf16[256,64]{0,1:T(8,128)(2,1)}, u32[]{:S(2)}) copy-start(bf16[256,64]{0,1:T(8,128)(2,1)} %param.9) | copy-start | bytes 98308
  3.9 16.5 %collective-permute-start = (bf16[400,128]{1,0:T(8,128)(2,1)S(1)}, bf16[400,128]{1,0:T(8,128)(2,1)S(1)}, u32[]{:S(2)}, u32[]{:S(2)}) collective-permute-start(bf16[400,128]{1,0:T(8,128)(2,1)S(1)} %get-tuple-element.19), channel_id=1, source_target_pairs={{0,1},{1,0},{2,3},{3,2},{4,5},{5,4},{6,7},{7,6},{8,9},{9,8},{10,11... | collective-permute-start | bytes 307208 | tf_op jit(solution)/shard_map/ppermute | solution.py:21
  6.9 3.9 %collective-permute-start.1 = (bf16[64,256]{1,0:T(8,128)(2,1)S(1)}, bf16[64,256]{1,0:T(8,128)(2,1)S(1)}, u32[]{:S(2)}, u32[]{:S(2)}) collective-permute-start(bf16[64,256]{1,0:T(8,128)(2,1)S(1)} %bitcast.4), channel_id=1, source_target_pairs={{0,1},{1,0},{2,3},{3,2},{4,5},{5,4},{6,7},{7,6},{8,9},{9,8},{10,11... | collective-permute-start | bytes 98312 | tf_op jit(solution)/shard_map/ppermute | solution.py:21
  11.6 6.9 %collective-permute-start.5 = (bf16[256,128]{1,0:T(8,128)(2,1)S(1)}, bf16[256,128]{1,0:T(8,128)(2,1)S(1)}, u32[]{:S(2)}, u32[]{:S(2)}) collective-permute-start(bf16[256,128]{1,0:T(8,128)(2,1)S(1)} %shard_map.121.refs_7_), channel_id=1, source_target_pairs={{0,16},{2,18},{4,20},{6,22},{8,24},{10,26},{12,28},{14,30},{16,0},... | collective-permute-start | bytes 196616 | tf_op jit(solution)/shard_map/ppermute | solution.py:21
  15.6 4.3 %collective-permute-start.4 = (bf16[256,128]{1,0:T(8,128)(2,1)S(1)}, bf16[256,128]{1,0:T(8,128)(2,1)S(1)}, u32[]{:S(2)}, u32[]{:S(2)}) collective-permute-start(bf16[256,128]{1,0:T(8,128)(2,1)S(1)} %shard_map.121.refs_7_), channel_id=1, source_target_pairs={{0,8},{2,10},{4,12},{6,14},{8,0},{10,2},{12,4},{14,6},{16,24},{18,... | collective-permute-start | bytes 196616 | tf_op jit(solution)/shard_map/ppermute | solution.py:21
  16.1 4.3 %collective-permute-start.3 = (bf16[256,128]{1,0:T(8,128)(2,1)S(1)}, bf16[256,128]{1,0:T(8,128)(2,1)S(1)}, u32[]{:S(2)}, u32[]{:S(2)}) collective-permute-start(bf16[256,128]{1,0:T(8,128)(2,1)S(1)} %shard_map.121.refs_7_), channel_id=1, source_target_pairs={{0,4},{2,6},{4,0},{6,2},{8,12},{10,14},{12,8},{14,10},{16,20},{18,... | collective-permute-start | bytes 196616 | tf_op jit(solution)/shard_map/ppermute | solution.py:21
  17.6 2.8 %collective-permute-start.2 = (bf16[256,128]{1,0:T(8,128)(2,1)S(1)}, bf16[256,128]{1,0:T(8,128)(2,1)S(1)}, u32[]{:S(2)}, u32[]{:S(2)}) collective-permute-start(bf16[256,128]{1,0:T(8,128)(2,1)S(1)} %shard_map.121.refs_7_), channel_id=1, source_target_pairs={{0,2},{2,0},{4,6},{6,4},{8,10},{10,8},{12,14},{14,12},{16,18},{18,... | collective-permute-start | bytes 196616 | tf_op jit(solution)/shard_map/ppermute | solution.py:21
  22.4 1.3 %collective-permute-start.6 = (f32[136,128]{1,0:T(8,128)S(1)}, f32[136,128]{1,0:T(8,128)S(1)}, u32[]{:S(2)}, u32[]{:S(2)}) collective-permute-start(f32[136,128]{1,0:T(8,128)S(1)} %get-tuple-element.21.own), channel_id=1, source_target_pairs={{0,2},{2,0},{4,6},{6,4},{8,10},{10,8},{12,14},{14,12},{16,18},{18,... | collective-permute-start | bytes 208904 | tf_op jit(solution)/shard_map/ppermute | solution.py:21
  23.7 4.4 %collective-permute-start.7 = (f32[136,128]{1,0:T(8,128)S(1)}, f32[136,128]{1,0:T(8,128)S(1)}, u32[]{:S(2)}, u32[]{:S(2)}) collective-permute-start(f32[136,128]{1,0:T(8,128)S(1)} %shard_map.123.own), channel_id=1, source_target_pairs={{0,4},{2,6},{4,0},{6,2},{8,12},{10,14},{12,8},{14,10},{16,20},{18,... | collective-permute-start | bytes 208904 | tf_op jit(solution)/shard_map/ppermute | solution.py:21
  28.1 4.4 %collective-permute-start.8 = (f32[136,128]{1,0:T(8,128)S(1)}, f32[136,128]{1,0:T(8,128)S(1)}, u32[]{:S(2)}, u32[]{:S(2)}) collective-permute-start(f32[136,128]{1,0:T(8,128)S(1)} %shard_map.124.own), channel_id=1, source_target_pairs={{0,8},{2,10},{4,12},{6,14},{8,0},{10,2},{12,4},{14,6},{16,24},{18,... | collective-permute-start | bytes 208904 | tf_op jit(solution)/shard_map/ppermute | solution.py:21
  32.5 11.4 %collective-permute-start.9 = (f32[136,128]{1,0:T(8,128)S(1)}, f32[136,128]{1,0:T(8,128)S(1)}, u32[]{:S(2)}, u32[]{:S(2)}) collective-permute-start(f32[136,128]{1,0:T(8,128)S(1)} %shard_map.125.own), channel_id=1, source_target_pairs={{0,16},{2,18},{4,20},{6,22},{8,24},{10,26},{12,28},{14,30},{16,0},... | collective-permute-start | bytes 208904 | tf_op jit(solution)/shard_map/ppermute | solution.py:21
  33.3 4.8 %collective-permute-start.10 = (f32[64,256]{1,0:T(8,128)S(1)}, f32[64,256]{1,0:T(8,128)S(1)}, u32[]{:S(2)}, u32[]{:S(2)}) collective-permute-start(f32[64,256]{1,0:T(8,128)S(1)} %get-tuple-element.26), channel_id=1, source_target_pairs={{0,2},{2,0},{4,6},{6,4},{8,10},{10,8},{12,14},{14,12},{16,18},{18,... | collective-permute-start | bytes 196616 | tf_op jit(solution)/shard_map/ppermute | solution.py:21
  33.4 4.8 %collective-permute-start.11 = (f32[64,256]{1,0:T(8,128)S(1)}, f32[64,256]{1,0:T(8,128)S(1)}, u32[]{:S(2)}, u32[]{:S(2)}) collective-permute-start(f32[64,256]{1,0:T(8,128)S(1)} %get-tuple-element.27), channel_id=1, source_target_pairs={{0,4},{2,6},{4,0},{6,2},{8,12},{10,14},{12,8},{14,10},{16,20},{18,... | collective-permute-start | bytes 196616 | tf_op jit(solution)/shard_map/ppermute | solution.py:21
  34.9 4.3 %collective-permute-start.12 = (f32[64,256]{1,0:T(8,128)S(1)}, f32[64,256]{1,0:T(8,128)S(1)}, u32[]{:S(2)}, u32[]{:S(2)}) collective-permute-start(f32[64,256]{1,0:T(8,128)S(1)} %get-tuple-element.28), channel_id=1, source_target_pairs={{0,8},{2,10},{4,12},{6,14},{8,0},{10,2},{12,4},{14,6},{16,24},{18,... | collective-permute-start | bytes 196616 | tf_op jit(solution)/shard_map/ppermute | solution.py:21
  36.3 6.3 %collective-permute-start.13 = (f32[64,256]{1,0:T(8,128)S(1)}, f32[64,256]{1,0:T(8,128)S(1)}, u32[]{:S(2)}, u32[]{:S(2)}) collective-permute-start(f32[64,256]{1,0:T(8,128)S(1)} %get-tuple-element.29), channel_id=1, source_target_pairs={{0,16},{2,18},{4,20},{6,22},{8,24},{10,26},{12,28},{14,30},{16,0},... | collective-permute-start | bytes 196616 | tf_op jit(solution)/shard_map/ppermute | solution.py:21
where the time goes:
time: 44.8 us; the launch traced here: 44.5 us
  waiting for transfers between devices  18 us (40%)
  starting transfers between devices  17.6 us (39%)
  Pallas kernels  7.57 us (17%)
  between operations  1.42 us (3%)
    ppermute x14, waiting for transfers between devices, partner(): lax.ppermute(shard, axis, [(i, i ^ 1 << bit) for i in range(lax.axis_size...  18 us
    ppermute x14, starting transfers between devices, partner(): lax.ppermute(shard, axis, [(i, i ^ 1 << bit) for i in range(lax.axis_size...  17.6 us
    pallas_call x9, Pallas kernels, kernel_call(): pl.pallas_call(kernel, out_shape=out_shape, in_specs=in_specs, out_specs=...  7.57 us
  transfers between devices with their start and end apart: 14, of which 9 were waited for; matrix products, arithmetic and copies ran while one was open for 0% of the time, Pallas kernels for 5%

commit v1 on v0

v1 whole, which is shorter than its diff:
```python
import functools
import math

import jax
import jax.numpy as jnp
from jax import lax
from jax.experimental import pallas as pl
from jax.experimental.pallas import tpu as pltpu
from jax.sharding import PartitionSpec as P


TILE_GROUP, UNROLL = 16, 4
F32, BF16 = jnp.float32, jnp.bfloat16
VMEM = pl.BlockSpec(memory_space=pltpu.VMEM)
SMEM = pl.BlockSpec(memory_space=pltpu.SMEM)
HBM = pl.BlockSpec(memory_space=pltpu.HBM)


def partner(shard, axis, bit):
    return lax.ppermute(shard, axis, [(i, i ^ 1 << bit) for i in range(lax.axis_size(axis))])


def near(array):
    return pltpu.with_memory_space_constraint(array, pltpu.VMEM)


def kernel_call(kernel, out_shape, in_specs, args, out_specs=None, scratch=()):
    args = [near(arg) if spec is VMEM else arg for spec, arg in zip(in_specs, args, strict=True)]
    outs = jax.tree.map(lambda _: VMEM, out_shape, is_leaf=lambda x: hasattr(x, "shape"))
    return pl.pallas_call(
        kernel,
        out_shape=out_shape,
        in_specs=in_specs,
        out_specs=outs if out_specs is None else out_specs,
        scratch_shapes=list(scratch),
    )(*args)


def near_out(shape, dtype):
    return pltpu.VMEM(shape, dtype)


def dot(a, b, contract=(1, 0)):
    return lax.dot_general(
        a, b, (((contract[0],), (contract[1],)), ((), ())), preferred_element_type=F32
    )


def quotient(value, divisor):
    if divisor & (divisor - 1) == 0:
        return jnp.right_shift(value, divisor.bit_length() - 1)
    return lax.div(value, divisor)


def build_kernel(levels, clusters, *refs):
    tiles, src_far, dst_far, count_far, size_far, gout, weight, bias_far, own_far = refs[:9]
    hi, lo, pack, live, live_row, own = refs[9:15]
    acc, held, src, dst, count, size, sems, bias, side = refs[15:]
    slots, width = tiles.shape[0], tiles.shape[1]
    rows, _ = gout.shape
    feats = weight.shape[0]
    columns = hi.shape[1]
    scalars = [
        pltpu.make_async_copy(far, close, side.at[n])
        for n, (far, close) in enumerate(
            ((src_far, src), (dst_far, dst), (count_far, count), (size_far, size))
        )
    ]
    for copy in scalars:
        copy.start()
    starts = list(range(0, slots, TILE_GROUP))
    fetches = [
        pltpu.make_async_copy(
            tiles.at[pl.ds(first, min(TILE_GROUP, slots - first))],
            held.at[pl.ds(first, min(TILE_GROUP, slots - first))],
            sems.at[first // TILE_GROUP],
        )
        for first in starts
    ]
    for copy in fetches:
        copy.start()
    sides = (
        pltpu.make_async_copy(gout, pack.at[pl.ds(0, rows)], side.at[4]),
        pltpu.make_async_copy(weight, pack.at[pl.ds(rows, feats)], side.at[5]),
        pltpu.make_async_copy(bias_far, bias, side.at[6]),
        pltpu.make_async_copy(own_far, own, side.at[7]),
    )
    for copy in sides:
        copy.start()
    acc[...] = jnp.zeros_like(acc)
    for copy in scalars:
        copy.wait()
    node = lax.broadcasted_iota(jnp.int32, (width, live.shape[1]), 0)
    across = lax.broadcasted_iota(jnp.int32, (live_row.shape[0], width), 1)
    for c in range(clusters):
        live[pl.ds(c * width, width), :] = (node < size[c]).astype(F32)
        live_row[:, pl.ds(c * width, width)] = (across < size[c]).astype(F32)
    used = count[0, 0]
    me = lax.axis_index("rows")

    def block_of(slot):
        at = jnp.minimum(slot, slots - 1)
        source = src[at]
        group = quotient(source, clusters)
        differs = jnp.bitwise_xor(group, me)
        column = source - group * clusters
        for bit in range(levels):
            column = column + jnp.where(differs == 1 << bit, (bit + 1) * clusters, 0)
        column = jnp.where(slot < used, column, columns // width)
        row = jnp.where(slot < used, dst[at], 0)
        return at, (
            pl.ds(pl.multiple_of(row * width, width), width),
            pl.ds(pl.multiple_of(column * width, width), width),
        )

    def step(turn, carry):
        blocks = [block_of(turn * UNROLL + k) for k in range(UNROLL)]
        for slot, block in blocks:
            acc[block] = acc[block] + held[slot].astype(F32)
        return carry

    for first, copy in zip(starts, fetches):
        copy.wait()
        last = jnp.minimum(min(first + TILE_GROUP, slots), used)
        lax.fori_loop(first // UNROLL, quotient(last + UNROLL - 1, UNROLL), step, 0)
    total = acc[:, pl.ds(0, columns)]
    high = total.astype(BF16)
    hi[...] = high
    lo[...] = (total - high.astype(F32)).astype(BF16)
    for copy in sides:
        copy.wait()
    pack[pl.ds(rows + feats, 16), :] = thirds(bias[...])


def merge_kernel(own, other, live, out):
    mine, theirs = own[...].astype(F32), other[...].astype(F32)
    first = lax.axis_index("cols") == 0
    both = jnp.concatenate(
        [jnp.where(first, mine, theirs), jnp.where(first, theirs, mine)], axis=0
    )
    out[...] = (both.T * live[...]).astype(BF16)


def dense(agg, pack, live):
    nodes, feats = agg.shape
    shift = pack[pl.ds(nodes + feats, 16), :].astype(F32)
    pre = dot(agg, pack[pl.ds(nodes, feats), :]) + (shift[0:1] + shift[1:2] + shift[2:3])
    sig = jax.nn.sigmoid(pre)
    grad = pack[pl.ds(0, nodes), :].astype(F32) * sig * (1.0 + pre * (1.0 - sig)) * live
    return pre * sig * live, grad.astype(BF16)


def thirds(value):
    top = value.astype(BF16).astype(F32)
    middle = (value - top).astype(BF16).astype(F32)
    row = lax.broadcasted_iota(jnp.int32, (16, value.shape[1]), 0)
    parts = jnp.where(row == 0, top, jnp.where(row == 1, middle, jnp.where(row == 2, value - top - middle, 0.0)))
    return parts.astype(BF16)


def main_kernel(levels, hi, lo, pack, live, *refs):
    tables = refs[: levels + 1]
    sums, agg_out, grad_pre_out, hidden_out = refs[levels + 1 :]
    nodes, feats = tables[0].shape
    agg = jnp.zeros((nodes, feats), F32)
    for level, table in enumerate(tables):
        value = table[...]
        at = (slice(None), pl.ds(level * nodes, nodes))
        agg = agg + dot(hi[at], value) + dot(lo[at], value)
    agg = agg.astype(BF16)
    hidden, grad_pre = dense(agg, pack, live[...])
    sums[pl.ds(0, feats), :] = dot(agg, grad_pre, (0, 0)).astype(BF16)
    sums[pl.ds(feats, 16), :] = thirds(jnp.sum(grad_pre.astype(F32), axis=0, keepdims=True))
    agg_out[...] = agg
    grad_pre_out[...] = grad_pre
    hidden_out[...] = hidden.astype(BF16)


def spread_kernel(levels, hi, lo, agg, grad_pre, hidden, own, pack, live, *refs):
    hidden_out, outs, sem = refs[0], refs[1:-1], refs[-1]
    leave = pltpu.make_async_copy(hidden, hidden_out, sem)
    leave.start()
    nodes, _ = agg.shape
    half = outs[0].shape[0]
    _, grad_other = dense(agg[...], pack, live[...])
    mine = pl.ds(pl.multiple_of(nodes + lax.axis_index("cols") * half, half), half)
    value = dot(own[mine, :], grad_pre[...], (1, 1)) + dot(pack[mine, :], grad_other, (1, 1))
    value = value.astype(BF16)
    for level in range(levels + 1):
        at = (slice(None), pl.ds(level * nodes, nodes))
        outs[level][...] = (dot(value, hi[at]) + dot(value, lo[at])).astype(outs[level].dtype)
    leave.wait()


def finish_kernel(live_row, *refs):
    total = refs[0][...]
    for part in refs[1:-1]:
        total = total + part[...].astype(F32)
    refs[-1][...] = (total * live_row[0:1, :]).astype(BF16)


def add_kernel(own, other, out):
    if own.dtype == F32:
        out[...] = own[...] + other[...]
    else:
        feats = own.shape[0] - 16
        total = own[...].astype(F32) + other[...].astype(F32)
        out[pl.ds(0, feats), :] = total[:feats]
        row = total[feats : feats + 1] + total[feats + 1 : feats + 2] + total[feats + 2 : feats + 3]
        out[pl.ds(feats, 8), :] = jnp.broadcast_to(row, (8, row.shape[1]))


def add(own, other):
    rows, columns = own.shape
    shape = (rows if own.dtype == F32 else rows - 8, columns)
    return kernel_call(add_kernel, near_out(shape, F32), [VMEM, VMEM], (own, other))


def scale_kernel(scale, own, other, grad_weight, grad_bias):
    feats = grad_weight.shape[0]
    grad_weight[...] = (own[pl.ds(0, feats), :] + other[pl.ds(0, feats), :]) * scale
    grad_bias[...] = (own[pl.ds(feats, 1), :] + other[pl.ds(feats, 1), :]) * scale


def local(features, adj_tiles, tile_src, tile_dst, tile_count, cluster_size, weight, bias, grad_out):
    clusters = cluster_size.shape[0]
    slots, width = adj_tiles.shape[:2]
    nodes, half = features.shape
    feats, hidden = weight.shape
    levels = lax.axis_size("rows").bit_length() - 1
    columns = (levels + 1) * nodes
    bias = bias.reshape(1, hidden)
    own = features.T
    other = partner(own, "cols", 0)
    hi, lo, pack, live, live_row, own = kernel_call(
        functools.partial(build_kernel, levels, clusters),
        (
            near_out((nodes, columns), BF16),
            near_out((nodes, columns), BF16),
            near_out((nodes + feats + 16, hidden), BF16),
            near_out((nodes, hidden), F32),
            near_out((8, nodes), F32),
            near_out((half, nodes), BF16),
        ),
        [HBM] * 9,
        (adj_tiles, tile_src, tile_dst, tile_count.reshape(1, 1), cluster_size, grad_out, weight, bias, own),
        scratch=[
            pltpu.VMEM((nodes, columns + width), F32),
            pltpu.VMEM((slots, width, width), BF16),
            pltpu.SMEM((slots,), jnp.int32),
            pltpu.SMEM((slots,), jnp.int32),
            pltpu.SMEM((1, 1), jnp.int32),
            pltpu.SMEM((clusters,), jnp.int32),
            pltpu.SemaphoreType.DMA((-(-slots // TILE_GROUP),)),
            pltpu.VMEM((1, hidden), F32),
            pltpu.SemaphoreType.DMA((8,)),
        ],
    )
    table = kernel_call(merge_kernel, near_out((nodes, feats), BF16), [VMEM, VMEM, VMEM], (own, other, live))
    tables = [table]
    for bit in range(levels):
        tables.append(partner(table, "rows", bit))
    other_pack = partner(pack, "cols", 0)
    sums, agg, grad_pre, hidden_near = kernel_call(
        functools.partial(main_kernel, levels),
        (
            near_out((feats + 16, hidden), BF16),
            near_out((nodes, feats), BF16),
            near_out((nodes, hidden), BF16),
            near_out((nodes, hidden), BF16),
        ),
        [VMEM] * (levels + 5),
        (hi, lo, pack, live, *tables),
    )
    hidden_out, *parts = kernel_call(
        functools.partial(spread_kernel, levels),
        [jax.ShapeDtypeStruct((nodes, hidden), BF16), near_out((half, nodes), F32)]
        + [near_out((half, nodes), BF16)] * levels,
        [VMEM] * 8,
        (hi, lo, agg, grad_pre, hidden_near, pack, other_pack, live),
        out_specs=[HBM] + [VMEM] * (levels + 1),
        scratch=[pltpu.SemaphoreType.DMA],
    )
    received = []
    for bit in range(levels):
        received.append(partner(parts[bit + 1], "rows", bit))
    moved = None
    for turn in range(levels):
        sums = add(sums, moved) if turn else sums
        moved = partner(sums, "rows", levels - 1 - turn)
    grad_features = kernel_call(
        finish_kernel, jax.ShapeDtypeStruct((half, nodes), BF16), [VMEM] * (levels + 2), (live_row, parts[0], *received)
    )
    grad_scale = 1.0 / math.sqrt(nodes * lax.axis_size("rows"))
    grad_weight, grad_bias = kernel_call(
        functools.partial(scale_kernel, grad_scale),
        (
            jax.ShapeDtypeStruct((feats, hidden), F32),
            jax.ShapeDtypeStruct((1, hidden), F32),
        ),
        [VMEM, VMEM],
        (sums, moved),
    )
    return (hidden_out, grad_weight, grad_bias.reshape(hidden), grad_features.T)


def solution(mesh):
    return jax.shard_map(
        local,
        mesh=mesh,
        in_specs=(
            P("rows", "cols"),
            P("rows", None, None),
            P("rows"),
            P("rows"),
            P("rows"),
            P("rows"),
            P(None, "cols"),
            P("cols"),
            P("rows", "cols"),
        ),
        out_specs=(P("rows", "cols"), P(None, "cols"), P("cols"), P("rows", "cols")),
        check_vma=False,
    )
```

time: 44.8 us -> 41.1 us (0.917)
  Pallas kernels: 7.57 us -> 5.24 us
  waiting for transfers between devices: 18 us -> 16.7 us
    pallas_call x9, Pallas kernels: 7.57 us -> 5.24 us  [kernel_call(): pl.pallas_call(kernel, out_shape=out_shape, in_specs=in_specs, out_specs=...]
    ppermute x14, waiting for transfers between devices: 18 us -> 16.7 us  [partner(): lax.ppermute(shard, axis, [(i, i ^ 1 << bit) for i in range(lax.axis_size...]
  transfers between devices with their start and end apart: 14 -> 14, of which waited for: 9 -> 8; matrix products, arithmetic and copies ran while one was open for 0% -> 0% of each run, Pallas kernels for 5% -> 9%
where the time goes in v1:
time: 41.1 us; the launch traced here: 41 us
  starting transfers between devices  17.7 us (43%)
  waiting for transfers between devices  16.7 us (41%)
  Pallas kernels  5.24 us (13%)
  between operations  1.37 us (3%)
    ppermute x14, starting transfers between devices, partner(): lax.ppermute(shard, axis, [(i, i ^ 1 << bit) for i in range(lax.axis_size...  17.7 us
    ppermute x14, waiting for transfers between devices, partner(): lax.ppermute(shard, axis, [(i, i ^ 1 << bit) for i in range(lax.axis_size...  16.7 us
    pallas_call x9, Pallas kernels, kernel_call(): pl.pallas_call(kernel, out_shape=out_shape, in_specs=in_specs, out_specs=...  5.24 us
  transfers between devices with their start and end apart: 14, of which 8 were waited for; matrix products, arithmetic and copies ran while one was open for 0% of the time, Pallas kernels for 9%

profile of v1, /device:TPU:0, one launch (start us, length us, event | category | flops | bytes accessed | tf_op | source)
XLA Modules:
  0.0 41.0 jit_solution(10703573634662492005)
XLA Ops:
  0.6 3.0 %collective-permute-start = (bf16[64,256]{1,0:T(8,128)(2,1)}, bf16[64,256]{1,0:T(8,128)(2,1)S(1)}, u32[]{:S(2)}, u32[]{:S(2)}) collective-permute-start(bf16[64,256]{1,0:T(8,128)(2,1)} %bitcast.6), channel_id=1, source_target_pairs={{0,1},{1,0},{2,3},{3,2},{4,5},{5,4},{6,7},{7,6},{8,9},{9,8},{10,11... | collective-permute-start | bytes 98312 | tf_op jit(solution)/shard_map/ppermute | solution.py:20
  4.3 2.2 %shard_map.120 = (bf16[256,1280]{1,0:T(8,128)(2,1)S(1)}, bf16[256,1280]{1,0:T(8,128)(2,1)S(1)}, bf16[400,128]{1,0:T(8,128)(2,1)S(1)}, f32[256,128]{1,0:T(8,128)S...) custom-call(bf16[96,128,128]{2,1,0:T(8,128)(2,1)} %refs_0_.1, s32[96]{0:T(128)} %refs_1_.1, s32[96]{0:T(128)} %refs_2_.1, ...), custom_call_target="tpu_custom_call" | custom-call | tf_op jit(solution)/shard_map/pallas_call | solution.py:30
  6.6 0.1 shard_map.121.refs_0_
  6.8 1.6 %collective-permute-start.2 = (bf16[256,128]{1,0:T(8,128)(2,1)S(1)}, bf16[256,128]{1,0:T(8,128)(2,1)S(1)}, u32[]{:S(2)}, u32[]{:S(2)}) collective-permute-start(bf16[256,128]{1,0:T(8,128)(2,1)S(1)} %shard_map.121.refs_0_), channel_id=1, source_target_pairs={{0,4},{2,6},{4,0},{6,2},{8,12},{10,14},{12,8},{14,10},{16,20},{18,... | collective-permute-start | bytes 196616 | tf_op jit(solution)/shard_map/ppermute | solution.py:20
  8.3 1.6 %collective-permute-start.3 = (bf16[256,128]{1,0:T(8,128)(2,1)S(1)}, bf16[256,128]{1,0:T(8,128)(2,1)S(1)}, u32[]{:S(2)}, u32[]{:S(2)}) collective-permute-start(bf16[256,128]{1,0:T(8,128)(2,1)S(1)} %shard_map.121.refs_0_), channel_id=1, source_target_pairs={{0,8},{2,10},{4,12},{6,14},{8,0},{10,2},{12,4},{14,6},{16,24},{18,... | collective-permute-start | bytes 196616 | tf_op jit(solution)/shard_map/ppermute | solution.py:20
  9.9 2.6 %collective-permute-start.4 = (bf16[256,128]{1,0:T(8,128)(2,1)S(1)}, bf16[256,128]{1,0:T(8,128)(2,1)S(1)}, u32[]{:S(2)}, u32[]{:S(2)}) collective-permute-start(bf16[256,128]{1,0:T(8,128)(2,1)S(1)} %shard_map.121.refs_0_), channel_id=1, source_target_pairs={{0,16},{2,18},{4,20},{6,22},{8,24},{10,26},{12,28},{14,30},{16,0},... | collective-permute-start | bytes 196616 | tf_op jit(solution)/shard_map/ppermute | solution.py:20
  12.5 0.1 collective-permute-done.3.refs_3_
  12.6 3.5 %collective-permute-done.4.refs_4_ = bf16[256,128]{1,0:T(8,128)(2,1)S(1)} collective-permute-done((bf16[256,128]{1,0:T(8,128)(2,1)S(1)}, bf16[256,128]{1,0:T(8,128)(2,1)S(1)}, u32[]{:S(2)}, u32[]{:S(2)}) %collective-permute-start.4) | collective-permute-done | bytes 65568 | tf_op jit(solution)/shard_map/ppermute | solution.py:20
  16.1 0.8 %shard_map.122 = (bf16[144,128]{1,0:T(8,128)(2,1)S(1)}, bf16[256,128]{1,0:T(8,128)(2,1)S(1)}, bf16[256,128]{1,0:T(8,128)(2,1)S(1)}, bf16[256,128]{1,0:T(8,128)(2,1)S(1)}) custom-call(bf16[256,1280]{1,0:T(8,128)(2,1)S(1)} %get-tuple-element.22.hi, bf16[256,1280]{1,0:T(8,128)(2,1)S(1)} %get-tuple-element.23.lo, ...), custom_call_target="tpu_custom_call" | custom-call | tf_op jit(solution)/shard_map/pallas_call | solution.py:30
  16.9 1.6 %collective-permute-start.6 = (bf16[144,128]{1,0:T(8,128)(2,1)S(1)}, bf16[144,128]{1,0:T(8,128)(2,1)S(1)}, u32[]{:S(2)}, u32[]{:S(2)}) collective-permute-start(bf16[144,128]{1,0:T(8,128)(2,1)S(1)} %get-tuple-element.31.own), channel_id=1, source_target_pairs={{0,16},{2,18},{4,20},{6,22},{8,24},{10,26},{12,28},{14,30},{16,0},... | collective-permute-start | bytes 110600 | tf_op jit(solution)/shard_map/ppermute | solution.py:20
  18.5 3.6 %collective-permute-done.6.other = bf16[144,128]{1,0:T(8,128)(2,1)S(1)} collective-permute-done((bf16[144,128]{1,0:T(8,128)(2,1)S(1)}, bf16[144,128]{1,0:T(8,128)(2,1)S(1)}, u32[]{:S(2)}, u32[]{:S(2)}) %collective-permute-start.6) | collective-permute-done | bytes 36896 | tf_op jit(solution)/shard_map/ppermute | solution.py:20
  22.2 0.2 collective-permute-start.7
  22.3 4.2 %collective-permute-done.7.other = f32[136,128]{1,0:T(8,128)S(1)} collective-permute-done((f32[136,128]{1,0:T(8,128)S(1)}, f32[136,128]{1,0:T(8,128)S(1)}, u32[]{:S(2)}, u32[]{:S(2)}) %collective-permute-start.7) | collective-permute-done | bytes 69664 | tf_op jit(solution)/shard_map/ppermute | solution.py:20
  26.6 1.7 %collective-permute-start.5 = (bf16[400,128]{1,0:T(8,128)(2,1)S(1)}, bf16[400,128]{1,0:T(8,128)(2,1)S(1)}, u32[]{:S(2)}, u32[]{:S(2)}) collective-permute-start(bf16[400,128]{1,0:T(8,128)(2,1)S(1)} %get-tuple-element.24.pack.own), channel_id=1, source_target_pairs={{0,1},{1,0},{2,3},{3,2},{4,5},{5,4},{6,7},{7,6},{8,9},{9,8},{10,11... | collective-permute-start | bytes 307208 | tf_op jit(solution)/shard_map/ppermute | solution.py:20
  28.4 2.6 %collective-permute-done.8.other = f32[136,128]{1,0:T(8,128)S(1)} collective-permute-done((f32[136,128]{1,0:T(8,128)S(1)}, f32[136,128]{1,0:T(8,128)S(1)}, u32[]{:S(2)}, u32[]{:S(2)}) %collective-permute-start.8) | collective-permute-done | bytes 69664 | tf_op jit(solution)/shard_map/ppermute | solution.py:20
  31.0 0.3 collective-permute-done.5.pack
  31.4 0.8 %shard_map.123 = (bf16[256,128]{1,0:T(8,128)(2,1)}, f32[64,256]{1,0:T(8,128)S(1)}, bf16[64,256]{1,0:T(8,128)(2,1)S(1)}, bf16[64,256]{1,0:T(8,128)(2,1)S(1)}, bf1...) custom-call(bf16[256,1280]{1,0:T(8,128)(2,1)S(1)} %get-tuple-element.22.hi, ...), custom_call_target="tpu_custom_call" | custom-call | tf_op jit(solution)/shard_map/pallas_call | solution.py:30
  32.2 0.2 collective-permute-start.10
  32.4 1.9 %collective-permute-start.11 = (bf16[64,256]{1,0:T(8,128)(2,1)S(1)}, bf16[64,256]{1,0:T(8,128)(2,1)S(1)}, u32[]{:S(2)}, u32[]{:S(2)}) collective-permute-start(bf16[64,256]{1,0:T(8,128)(2,1)S(1)} %get-tuple-element.37), channel_id=1, source_target_pairs={{0,4},{2,6},{4,0},{6,2},{8,12},{10,14},{12,8},{14,10},{16,20},{18,... | collective-permute-start | bytes 98312 | tf_op jit(solution)/shard_map/ppermute | solution.py:20
  34.4 3.1 %collective-permute-start.13 = (bf16[64,256]{1,0:T(8,128)(2,1)S(1)}, bf16[64,256]{1,0:T(8,128)(2,1)S(1)}, u32[]{:S(2)}, u32[]{:S(2)}) collective-permute-start(bf16[64,256]{1,0:T(8,128)(2,1)S(1)} %get-tuple-element.39), channel_id=1, source_target_pairs={{0,16},{2,18},{4,20},{6,22},{8,24},{10,26},{12,28},{14,30},{16,0},... | collective-permute-start | bytes 98312 | tf_op jit(solution)/shard_map/ppermute | solution.py:20
  37.5 0.8 %collective-permute-done.12.refs_3_ = bf16[64,256]{1,0:T(8,128)(2,1)S(1)} collective-permute-done((bf16[64,256]{1,0:T(8,128)(2,1)S(1)}, bf16[64,256]{1,0:T(8,128)(2,1)S(1)}, u32[]{:S(2)}, u32[]{:S(2)}) %collective-permute-start.12) | collective-permute-done | bytes 32800 | tf_op jit(solution)/shard_map/ppermute | solution.py:20
  38.2 1.5 %collective-permute-done.13.refs_4_ = bf16[64,256]{1,0:T(8,128)(2,1)S(1)} collective-permute-done((bf16[64,256]{1,0:T(8,128)(2,1)S(1)}, bf16[64,256]{1,0:T(8,128)(2,1)S(1)}, u32[]{:S(2)}, u32[]{:S(2)}) %collective-permute-start.13) | collective-permute-done | bytes 32800 | tf_op jit(solution)/shard_map/ppermute | solution.py:20
  39.7 0.6 %shard_map.128 = bf16[64,256]{1,0:T(8,128)(2,1)} custom-call(f32[8,256]{1,0:T(8,128)S(1)} %get-tuple-element.34.live_row, f32[64,256]{1,0:T(8,128)S(1)} %get-tuple-element.35.refs_0_, bf16[64,256]{1,0:T(8,128)(2,1)S(1)} %collective-permute-done.10.refs_1_, bf16[64,256]{1,0:T(8,128)(2,1)S(1)} %collective-permute-done.11.refs_2_, ...), custom_call_target="tpu_custom_call" | custom-call | tf_op jit(solution)/shard_map/pallas_call | solution.py:30
  40.3 0.6 %shard_map.127 = (f32[128,128]{1,0:T(8,128)}, f32[1,128]{1,0:T(1,128)}) custom-call(f32[136,128]{1,0:T(8,128)S(1)} %shard_map.126.own, f32[136,128]{1,0:T(8,128)S(1)} %collective-permute-done.9.other), custom_call_target="tpu_custom_call" | custom-call | tf_op jit(solution)/shard_map/pallas_call | solution.py:30
  (13 shorter events, 0.4 us)
Async XLA Ops:
  0.6 5.9 %collective-permute-start = (bf16[64,256]{1,0:T(8,128)(2,1)}, bf16[64,256]{1,0:T(8,128)(2,1)S(1)}, u32[]{:S(2)}, u32[]{:S(2)}) collective-permute-start(bf16[64,256]{1,0:T(8,128)(2,1)} %bitcast.6), channel_id=1, source_target_pairs={{0,1},{1,0},{2,3},{3,2},{4,5},{5,4},{6,7},{7,6},{8,9},{9,8},{10,11... | collective-permute-start | bytes 98312 | tf_op jit(solution)/shard_map/ppermute | solution.py:20
  6.7 5.8 %collective-permute-start.1 = (bf16[256,128]{1,0:T(8,128)(2,1)S(1)}, bf16[256,128]{1,0:T(8,128)(2,1)S(1)}, u32[]{:S(2)}, u32[]{:S(2)}) collective-permute-start(bf16[256,128]{1,0:T(8,128)(2,1)S(1)} %shard_map.121.refs_0_), channel_id=1, source_target_pairs={{0,2},{2,0},{4,6},{6,4},{8,10},{10,8},{12,14},{14,12},{16,18},{18,... | collective-permute-start | bytes 196616 | tf_op jit(solution)/shard_map/ppermute | solution.py:20
  6.8 5.8 %collective-permute-start.2 = (bf16[256,128]{1,0:T(8,128)(2,1)S(1)}, bf16[256,128]{1,0:T(8,128)(2,1)S(1)}, u32[]{:S(2)}, u32[]{:S(2)}) collective-permute-start(bf16[256,128]{1,0:T(8,128)(2,1)S(1)} %shard_map.121.refs_0_), channel_id=1, source_target_pairs={{0,4},{2,6},{4,0},{6,2},{8,12},{10,14},{12,8},{14,10},{16,20},{18,... | collective-permute-start | bytes 196616 | tf_op jit(solution)/shard_map/ppermute | solution.py:20
  8.3 4.3 %collective-permute-start.3 = (bf16[256,128]{1,0:T(8,128)(2,1)S(1)}, bf16[256,128]{1,0:T(8,128)(2,1)S(1)}, u32[]{:S(2)}, u32[]{:S(2)}) collective-permute-start(bf16[256,128]{1,0:T(8,128)(2,1)S(1)} %shard_map.121.refs_0_), channel_id=1, source_target_pairs={{0,8},{2,10},{4,12},{6,14},{8,0},{10,2},{12,4},{14,6},{16,24},{18,... | collective-permute-start | bytes 196616 | tf_op jit(solution)/shard_map/ppermute | solution.py:20
  9.9 6.2 %collective-permute-start.4 = (bf16[256,128]{1,0:T(8,128)(2,1)S(1)}, bf16[256,128]{1,0:T(8,128)(2,1)S(1)}, u32[]{:S(2)}, u32[]{:S(2)}) collective-permute-start(bf16[256,128]{1,0:T(8,128)(2,1)S(1)} %shard_map.121.refs_0_), channel_id=1, source_target_pairs={{0,16},{2,18},{4,20},{6,22},{8,24},{10,26},{12,28},{14,30},{16,0},... | collective-permute-start | bytes 196616 | tf_op jit(solution)/shard_map/ppermute | solution.py:20
  16.9 5.2 %collective-permute-start.6 = (bf16[144,128]{1,0:T(8,128)(2,1)S(1)}, bf16[144,128]{1,0:T(8,128)(2,1)S(1)}, u32[]{:S(2)}, u32[]{:S(2)}) collective-permute-start(bf16[144,128]{1,0:T(8,128)(2,1)S(1)} %get-tuple-element.31.own), channel_id=1, source_target_pairs={{0,16},{2,18},{4,20},{6,22},{8,24},{10,26},{12,28},{14,30},{16,0},... | collective-permute-start | bytes 110600 | tf_op jit(solution)/shard_map/ppermute | solution.py:20
  22.2 4.4 %collective-permute-start.7 = (f32[136,128]{1,0:T(8,128)S(1)}, f32[136,128]{1,0:T(8,128)S(1)}, u32[]{:S(2)}, u32[]{:S(2)}) collective-permute-start(f32[136,128]{1,0:T(8,128)S(1)} %shard_map.124.own), channel_id=1, source_target_pairs={{0,8},{2,10},{4,12},{6,14},{8,0},{10,2},{12,4},{14,6},{16,24},{18,... | collective-permute-start | bytes 208904 | tf_op jit(solution)/shard_map/ppermute | solution.py:20
  26.6 4.4 %collective-permute-start.8 = (f32[136,128]{1,0:T(8,128)S(1)}, f32[136,128]{1,0:T(8,128)S(1)}, u32[]{:S(2)}, u32[]{:S(2)}) collective-permute-start(f32[136,128]{1,0:T(8,128)S(1)} %shard_map.125.own), channel_id=1, source_target_pairs={{0,4},{2,6},{4,0},{6,2},{8,12},{10,14},{12,8},{14,10},{16,20},{18,... | collective-permute-start | bytes 208904 | tf_op jit(solution)/shard_map/ppermute | solution.py:20
  26.6 4.7 %collective-permute-start.5 = (bf16[400,128]{1,0:T(8,128)(2,1)S(1)}, bf16[400,128]{1,0:T(8,128)(2,1)S(1)}, u32[]{:S(2)}, u32[]{:S(2)}) collective-permute-start(bf16[400,128]{1,0:T(8,128)(2,1)S(1)} %get-tuple-element.24.pack.own), channel_id=1, source_target_pairs={{0,1},{1,0},{2,3},{3,2},{4,5},{5,4},{6,7},{7,6},{8,9},{9,8},{10,11... | collective-permute-start | bytes 307208 | tf_op jit(solution)/shard_map/ppermute | solution.py:20
  31.0 9.4 %collective-permute-start.9 = (f32[136,128]{1,0:T(8,128)S(1)}, f32[136,128]{1,0:T(8,128)S(1)}, u32[]{:S(2)}, u32[]{:S(2)}) collective-permute-start(f32[136,128]{1,0:T(8,128)S(1)} %shard_map.126.own), channel_id=1, source_target_pairs={{0,2},{2,0},{4,6},{6,4},{8,10},{10,8},{12,14},{14,12},{16,18},{18,... | collective-permute-start | bytes 208904 | tf_op jit(solution)/shard_map/ppermute | solution.py:20
  32.2 5.3 %collective-permute-start.10 = (bf16[64,256]{1,0:T(8,128)(2,1)S(1)}, bf16[64,256]{1,0:T(8,128)(2,1)S(1)}, u32[]{:S(2)}, u32[]{:S(2)}) collective-permute-start(bf16[64,256]{1,0:T(8,128)(2,1)S(1)} %get-tuple-element.36), channel_id=1, source_target_pairs={{0,2},{2,0},{4,6},{6,4},{8,10},{10,8},{12,14},{14,12},{16,18},{18,... | collective-permute-start | bytes 98312 | tf_op jit(solution)/shard_map/ppermute | solution.py:20
  32.4 5.0 %collective-permute-start.11 = (bf16[64,256]{1,0:T(8,128)(2,1)S(1)}, bf16[64,256]{1,0:T(8,128)(2,1)S(1)}, u32[]{:S(2)}, u32[]{:S(2)}) collective-permute-start(bf16[64,256]{1,0:T(8,128)(2,1)S(1)} %get-tuple-element.37), channel_id=1, source_target_pairs={{0,4},{2,6},{4,0},{6,2},{8,12},{10,14},{12,8},{14,10},{16,20},{18,... | collective-permute-start | bytes 98312 | tf_op jit(solution)/shard_map/ppermute | solution.py:20
  34.3 3.9 %collective-permute-start.12 = (bf16[64,256]{1,0:T(8,128)(2,1)S(1)}, bf16[64,256]{1,0:T(8,128)(2,1)S(1)}, u32[]{:S(2)}, u32[]{:S(2)}) collective-permute-start(bf16[64,256]{1,0:T(8,128)(2,1)S(1)} %get-tuple-element.38), channel_id=1, source_target_pairs={{0,8},{2,10},{4,12},{6,14},{8,0},{10,2},{12,4},{14,6},{16,24},{18,... | collective-permute-start | bytes 98312 | tf_op jit(solution)/shard_map/ppermute | solution.py:20
  34.4 5.3 %collective-permute-start.13 = (bf16[64,256]{1,0:T(8,128)(2,1)S(1)}, bf16[64,256]{1,0:T(8,128)(2,1)S(1)}, u32[]{:S(2)}, u32[]{:S(2)}) collective-permute-start(bf16[64,256]{1,0:T(8,128)(2,1)S(1)} %get-tuple-element.39), channel_id=1, source_target_pairs={{0,16},{2,18},{4,20},{6,22},{8,24},{10,26},{12,28},{14,30},{16,0},... | collective-permute-start | bytes 98312 | tf_op jit(solution)/shard_map/ppermute | solution.py:20

commit v2 on v1

--- a/solution.py
+++ b/solution.py
@@ -200,20 +200,20 @@
 
 
 def add_kernel(own, other, out):
-    if own.dtype == F32:
-        out[...] = own[...] + other[...]
+    feats = own.shape[0] - 16
+    total = own[...].astype(F32) + other[...].astype(F32)
+    row = total[feats : feats + 1] + total[feats + 1 : feats + 2] + total[feats + 2 : feats + 3]
+    out[pl.ds(0, feats), :] = total[:feats].astype(out.dtype)
+    if out.dtype == F32:
+        out[pl.ds(feats, 8), :] = jnp.broadcast_to(row, (8, row.shape[1]))
     else:
-        feats = own.shape[0] - 16
-        total = own[...].astype(F32) + other[...].astype(F32)
-        out[pl.ds(0, feats), :] = total[:feats]
-        row = total[feats : feats + 1] + total[feats + 1 : feats + 2] + total[feats + 2 : feats + 3]
-        out[pl.ds(feats, 8), :] = jnp.broadcast_to(row, (8, row.shape[1]))
-
-
-def add(own, other):
+        out[pl.ds(feats, 16), :] = thirds(row)
+
+
+def add(own, other, dtype):
     rows, columns = own.shape
-    shape = (rows if own.dtype == F32 else rows - 8, columns)
-    return kernel_call(add_kernel, near_out(shape, F32), [VMEM, VMEM], (own, other))
+    shape = (rows - 8 if dtype == F32 else rows, columns)
+    return kernel_call(add_kernel, near_out(shape, dtype), [VMEM, VMEM], (own, other))
 
 
 def scale_kernel(scale, own, other, grad_weight, grad_bias):
@@ -286,8 +286,9 @@
         received.append(partner(parts[bit + 1], "rows", bit))
     moved = None
     for turn in range(levels):
-        sums = add(sums, moved) if turn else sums
-        moved = partner(sums, "rows", levels - 1 - turn)
+        if turn:
+            sums = add(sums, moved, F32 if turn + 1 == levels else BF16)
+        moved = partner(sums, "rows", sum_bits(levels)[turn])
     grad_features = kernel_call(
         finish_kernel, jax.ShapeDtypeStruct((half, nodes), BF16), [VMEM] * (levels + 2), (live_row, parts[0], *received)
     )
@@ -302,6 +303,10 @@
         (sums, moved),
     )
     return (hidden_out, grad_weight, grad_bias.reshape(hidden), grad_features.T)
+
+
+def sum_bits(levels):
+    return list(reversed(range(levels)))
 
 
 def solution(mesh):

time: 41.1 us -> 39.1 us (0.951)
  starting transfers between devices: 17.7 us -> 16.3 us
  waiting for transfers between devices: 16.7 us -> 16 us
    ppermute x14, starting transfers between devices: 17.7 us -> 16.3 us  [partner(): lax.ppermute(shard, axis, [(i, i ^ 1 << bit) for i in range(lax.axis_size...]
    ppermute x14, waiting for transfers between devices: 16.7 us -> 16 us  [partner(): lax.ppermute(shard, axis, [(i, i ^ 1 << bit) for i in range(lax.axis_size...]
  transfers between devices with their start and end apart: 14 -> 14, of which waited for: 8 -> 7; matrix products, arithmetic and copies ran while one was open for 0% -> 0% of each run, Pallas kernels for 9% -> 10%
where the time goes in v2:
time: 39.1 us; the launch traced here: 38.9 us
  starting transfers between devices  16.3 us (42%)
  waiting for transfers between devices  16 us (41%)
  Pallas kernels  5.27 us (13%)
  between operations  1.37 us (4%)
    ppermute x14, starting transfers between devices, partner(): lax.ppermute(shard, axis, [(i, i ^ 1 << bit) for i in range(lax.axis_size...  16.3 us
    ppermute x14, waiting for transfers between devices, partner(): lax.ppermute(shard, axis, [(i, i ^ 1 << bit) for i in range(lax.axis_size...  16 us
    pallas_call x9, Pallas kernels, kernel_call(): pl.pallas_call(kernel, out_shape=out_shape, in_specs=in_specs, out_specs=...  5.27 us
  transfers between devices with their start and end apart: 14, of which 7 were waited for; matrix products, arithmetic and copies ran while one was open for 0% of the time, Pallas kernels for 10%

profile of v2, /device:TPU:0, one launch (start us, length us, event | category | flops | bytes accessed | tf_op | source)
XLA Modules:
  0.0 38.9 jit_solution(1627982363065185412)
XLA Ops:
  0.6 3.0 %collective-permute-start = (bf16[64,256]{1,0:T(8,128)(2,1)}, bf16[64,256]{1,0:T(8,128)(2,1)S(1)}, u32[]{:S(2)}, u32[]{:S(2)}) collective-permute-start(bf16[64,256]{1,0:T(8,128)(2,1)} %bitcast.6), channel_id=1, source_target_pairs={{0,1},{1,0},{2,3},{3,2},{4,5},{5,4},{6,7},{7,6},{8,9},{9,8},{10,11... | collective-permute-start | bytes 98312 | tf_op jit(solution)/shard_map/ppermute | solution.py:20
  4.3 2.2 %shard_map.120 = (bf16[256,1280]{1,0:T(8,128)(2,1)S(1)}, bf16[256,1280]{1,0:T(8,128)(2,1)S(1)}, bf16[400,128]{1,0:T(8,128)(2,1)S(1)}, f32[256,128]{1,0:T(8,128)S...) custom-call(bf16[96,128,128]{2,1,0:T(8,128)(2,1)} %refs_0_.1, s32[96]{0:T(128)} %refs_1_.1, s32[96]{0:T(128)} %refs_2_.1, ...), custom_call_target="tpu_custom_call" | custom-call | tf_op jit(solution)/shard_map/pallas_call | solution.py:30
  6.6 0.1 shard_map.121.refs_0_
  6.7 0.1 collective-permute-start.1
  6.8 1.6 %collective-permute-start.2 = (bf16[256,128]{1,0:T(8,128)(2,1)S(1)}, bf16[256,128]{1,0:T(8,128)(2,1)S(1)}, u32[]{:S(2)}, u32[]{:S(2)}) collective-permute-start(bf16[256,128]{1,0:T(8,128)(2,1)S(1)} %shard_map.121.refs_0_), channel_id=1, source_target_pairs={{0,4},{2,6},{4,0},{6,2},{8,12},{10,14},{12,8},{14,10},{16,20},{18,... | collective-permute-start | bytes 196616 | tf_op jit(solution)/shard_map/ppermute | solution.py:20
  8.3 1.6 %collective-permute-start.3 = (bf16[256,128]{1,0:T(8,128)(2,1)S(1)}, bf16[256,128]{1,0:T(8,128)(2,1)S(1)}, u32[]{:S(2)}, u32[]{:S(2)}) collective-permute-start(bf16[256,128]{1,0:T(8,128)(2,1)S(1)} %shard_map.121.refs_0_), channel_id=1, source_target_pairs={{0,8},{2,10},{4,12},{6,14},{8,0},{10,2},{12,4},{14,6},{16,24},{18,... | collective-permute-start | bytes 196616 | tf_op jit(solution)/shard_map/ppermute | solution.py:20
  9.9 2.6 %collective-permute-start.4 = (bf16[256,128]{1,0:T(8,128)(2,1)S(1)}, bf16[256,128]{1,0:T(8,128)(2,1)S(1)}, u32[]{:S(2)}, u32[]{:S(2)}) collective-permute-start(bf16[256,128]{1,0:T(8,128)(2,1)S(1)} %shard_map.121.refs_0_), channel_id=1, source_target_pairs={{0,16},{2,18},{4,20},{6,22},{8,24},{10,26},{12,28},{14,30},{16,0},... | collective-permute-start | bytes 196616 | tf_op jit(solution)/shard_map/ppermute | solution.py:20
  12.5 0.1 collective-permute-done.3.refs_3_
  12.6 3.5 %collective-permute-done.4.refs_4_ = bf16[256,128]{1,0:T(8,128)(2,1)S(1)} collective-permute-done((bf16[256,128]{1,0:T(8,128)(2,1)S(1)}, bf16[256,128]{1,0:T(8,128)(2,1)S(1)}, u32[]{:S(2)}, u32[]{:S(2)}) %collective-permute-start.4) | collective-permute-done | bytes 65568 | tf_op jit(solution)/shard_map/ppermute | solution.py:20
  16.1 0.8 %shard_map.122 = (bf16[144,128]{1,0:T(8,128)(2,1)S(1)}, bf16[256,128]{1,0:T(8,128)(2,1)S(1)}, bf16[256,128]{1,0:T(8,128)(2,1)S(1)}, bf16[256,128]{1,0:T(8,128)(2,1)S(1)}) custom-call(bf16[256,1280]{1,0:T(8,128)(2,1)S(1)} %get-tuple-element.22.hi, bf16[256,1280]{1,0:T(8,128)(2,1)S(1)} %get-tuple-element.23.lo, ...), custom_call_target="tpu_custom_call" | custom-call | tf_op jit(solution)/shard_map/pallas_call | solution.py:30
  16.9 1.6 %collective-permute-start.6 = (bf16[144,128]{1,0:T(8,128)(2,1)S(1)}, bf16[144,128]{1,0:T(8,128)(2,1)S(1)}, u32[]{:S(2)}, u32[]{:S(2)}) collective-permute-start(bf16[144,128]{1,0:T(8,128)(2,1)S(1)} %get-tuple-element.31.own), channel_id=1, source_target_pairs={{0,16},{2,18},{4,20},{6,22},{8,24},{10,26},{12,28},{14,30},{16,0},... | collective-permute-start | bytes 110600 | tf_op jit(solution)/shard_map/ppermute | solution.py:20
  18.5 3.6 %collective-permute-done.6.other = bf16[144,128]{1,0:T(8,128)(2,1)S(1)} collective-permute-done((bf16[144,128]{1,0:T(8,128)(2,1)S(1)}, bf16[144,128]{1,0:T(8,128)(2,1)S(1)}, u32[]{:S(2)}, u32[]{:S(2)}) %collective-permute-start.6) | collective-permute-done | bytes 36896 | tf_op jit(solution)/shard_map/ppermute | solution.py:20
  22.1 0.2 collective-permute-start.7
  22.3 1.2 %collective-permute-start.5 = (bf16[400,128]{1,0:T(8,128)(2,1)S(1)}, bf16[400,128]{1,0:T(8,128)(2,1)S(1)}, u32[]{:S(2)}, u32[]{:S(2)}) collective-permute-start(bf16[400,128]{1,0:T(8,128)(2,1)S(1)} %get-tuple-element.24.pack.own), channel_id=1, source_target_pairs={{0,1},{1,0},{2,3},{3,2},{4,5},{5,4},{6,7},{7,6},{8,9},{9,8},{10,11... | collective-permute-start | bytes 307208 | tf_op jit(solution)/shard_map/ppermute | solution.py:20
  23.6 2.6 %collective-permute-done.7.other = bf16[144,128]{1,0:T(8,128)(2,1)S(1)} collective-permute-done((bf16[144,128]{1,0:T(8,128)(2,1)S(1)}, bf16[144,128]{1,0:T(8,128)(2,1)S(1)}, u32[]{:S(2)}, u32[]{:S(2)}) %collective-permute-start.7) | collective-permute-done | bytes 36896 | tf_op jit(solution)/shard_map/ppermute | solution.py:20
  26.3 3.9 %collective-permute-done.8.other = bf16[144,128]{1,0:T(8,128)(2,1)S(1)} collective-permute-done((bf16[144,128]{1,0:T(8,128)(2,1)S(1)}, bf16[144,128]{1,0:T(8,128)(2,1)S(1)}, u32[]{:S(2)}, u32[]{:S(2)}) %collective-permute-start.8) | collective-permute-done | bytes 36896 | tf_op jit(solution)/shard_map/ppermute | solution.py:20
  30.3 0.8 %shard_map.123 = (bf16[256,128]{1,0:T(8,128)(2,1)}, f32[64,256]{1,0:T(8,128)S(1)}, bf16[64,256]{1,0:T(8,128)(2,1)S(1)}, bf16[64,256]{1,0:T(8,128)(2,1)S(1)}, bf1...) custom-call(bf16[256,1280]{1,0:T(8,128)(2,1)S(1)} %get-tuple-element.22.hi, ...), custom_call_target="tpu_custom_call" | custom-call | tf_op jit(solution)/shard_map/pallas_call | solution.py:30
  31.1 0.6 %collective-permute-start.10 = (bf16[64,256]{1,0:T(8,128)(2,1)S(1)}, bf16[64,256]{1,0:T(8,128)(2,1)S(1)}, u32[]{:S(2)}, u32[]{:S(2)}) collective-permute-start(bf16[64,256]{1,0:T(8,128)(2,1)S(1)} %get-tuple-element.36), channel_id=1, source_target_pairs={{0,2},{2,0},{4,6},{6,4},{8,10},{10,8},{12,14},{14,12},{16,18},{18,... | collective-permute-start | bytes 98312 | tf_op jit(solution)/shard_map/ppermute | solution.py:20
  31.7 1.1 %collective-permute-start.12 = (bf16[64,256]{1,0:T(8,128)(2,1)S(1)}, bf16[64,256]{1,0:T(8,128)(2,1)S(1)}, u32[]{:S(2)}, u32[]{:S(2)}) collective-permute-start(bf16[64,256]{1,0:T(8,128)(2,1)S(1)} %get-tuple-element.38), channel_id=1, source_target_pairs={{0,8},{2,10},{4,12},{6,14},{8,0},{10,2},{12,4},{14,6},{16,24},{18,... | collective-permute-start | bytes 98312 | tf_op jit(solution)/shard_map/ppermute | solution.py:20
  32.8 2.6 %collective-permute-start.13 = (bf16[64,256]{1,0:T(8,128)(2,1)S(1)}, bf16[64,256]{1,0:T(8,128)(2,1)S(1)}, u32[]{:S(2)}, u32[]{:S(2)}) collective-permute-start(bf16[64,256]{1,0:T(8,128)(2,1)S(1)} %get-tuple-element.39), channel_id=1, source_target_pairs={{0,16},{2,18},{4,20},{6,22},{8,24},{10,26},{12,28},{14,30},{16,0},... | collective-permute-start | bytes 98312 | tf_op jit(solution)/shard_map/ppermute | solution.py:20
  35.4 0.2 collective-permute-done.11.refs_2_
  35.6 2.0 %collective-permute-done.13.refs_4_ = bf16[64,256]{1,0:T(8,128)(2,1)S(1)} collective-permute-done((bf16[64,256]{1,0:T(8,128)(2,1)S(1)}, bf16[64,256]{1,0:T(8,128)(2,1)S(1)}, u32[]{:S(2)}, u32[]{:S(2)}) %collective-permute-start.13) | collective-permute-done | bytes 32800 | tf_op jit(solution)/shard_map/ppermute | solution.py:20
  37.6 0.6 %shard_map.128 = bf16[64,256]{1,0:T(8,128)(2,1)} custom-call(f32[8,256]{1,0:T(8,128)S(1)} %get-tuple-element.34.live_row, f32[64,256]{1,0:T(8,128)S(1)} %get-tuple-element.35.refs_0_, bf16[64,256]{1,0:T(8,128)(2,1)S(1)} %collective-permute-done.10.refs_1_, bf16[64,256]{1,0:T(8,128)(2,1)S(1)} %collective-permute-done.11.refs_2_, ...), custom_call_target="tpu_custom_call" | custom-call | tf_op jit(solution)/shard_map/pallas_call | solution.py:30
  38.3 0.6 %shard_map.127 = (f32[128,128]{1,0:T(8,128)}, f32[1,128]{1,0:T(1,128)}) custom-call(f32[136,128]{1,0:T(8,128)S(1)} %shard_map.126.own, f32[136,128]{1,0:T(8,128)S(1)} %collective-permute-done.9.other), custom_call_target="tpu_custom_call" | custom-call | tf_op jit(solution)/shard_map/pallas_call | solution.py:30
  (13 shorter events, 0.2 us)
Async XLA Ops:
  0.6 5.9 %collective-permute-start = (bf16[64,256]{1,0:T(8,128)(2,1)}, bf16[64,256]{1,0:T(8,128)(2,1)S(1)}, u32[]{:S(2)}, u32[]{:S(2)}) collective-permute-start(bf16[64,256]{1,0:T(8,128)(2,1)} %bitcast.6), channel_id=1, source_target_pairs={{0,1},{1,0},{2,3},{3,2},{4,5},{5,4},{6,7},{7,6},{8,9},{9,8},{10,11... | collective-permute-start | bytes 98312 | tf_op jit(solution)/shard_map/ppermute | solution.py:20
  6.7 5.8 %collective-permute-start.1 = (bf16[256,128]{1,0:T(8,128)(2,1)S(1)}, bf16[256,128]{1,0:T(8,128)(2,1)S(1)}, u32[]{:S(2)}, u32[]{:S(2)}) collective-permute-start(bf16[256,128]{1,0:T(8,128)(2,1)S(1)} %shard_map.121.refs_0_), channel_id=1, source_target_pairs={{0,2},{2,0},{4,6},{6,4},{8,10},{10,8},{12,14},{14,12},{16,18},{18,... | collective-permute-start | bytes 196616 | tf_op jit(solution)/shard_map/ppermute | solution.py:20
  6.8 5.8 %collective-permute-start.2 = (bf16[256,128]{1,0:T(8,128)(2,1)S(1)}, bf16[256,128]{1,0:T(8,128)(2,1)S(1)}, u32[]{:S(2)}, u32[]{:S(2)}) collective-permute-start(bf16[256,128]{1,0:T(8,128)(2,1)S(1)} %shard_map.121.refs_0_), channel_id=1, source_target_pairs={{0,4},{2,6},{4,0},{6,2},{8,12},{10,14},{12,8},{14,10},{16,20},{18,... | collective-permute-start | bytes 196616 | tf_op jit(solution)/shard_map/ppermute | solution.py:20
  8.3 4.3 %collective-permute-start.3 = (bf16[256,128]{1,0:T(8,128)(2,1)S(1)}, bf16[256,128]{1,0:T(8,128)(2,1)S(1)}, u32[]{:S(2)}, u32[]{:S(2)}) collective-permute-start(bf16[256,128]{1,0:T(8,128)(2,1)S(1)} %shard_map.121.refs_0_), channel_id=1, source_target_pairs={{0,8},{2,10},{4,12},{6,14},{8,0},{10,2},{12,4},{14,6},{16,24},{18,... | collective-permute-start | bytes 196616 | tf_op jit(solution)/shard_map/ppermute | solution.py:20
  9.9 6.2 %collective-permute-start.4 = (bf16[256,128]{1,0:T(8,128)(2,1)S(1)}, bf16[256,128]{1,0:T(8,128)(2,1)S(1)}, u32[]{:S(2)}, u32[]{:S(2)}) collective-permute-start(bf16[256,128]{1,0:T(8,128)(2,1)S(1)} %shard_map.121.refs_0_), channel_id=1, source_target_pairs={{0,16},{2,18},{4,20},{6,22},{8,24},{10,26},{12,28},{14,30},{16,0},... | collective-permute-start | bytes 196616 | tf_op jit(solution)/shard_map/ppermute | solution.py:20
  16.9 5.2 %collective-permute-start.6 = (bf16[144,128]{1,0:T(8,128)(2,1)S(1)}, bf16[144,128]{1,0:T(8,128)(2,1)S(1)}, u32[]{:S(2)}, u32[]{:S(2)}) collective-permute-start(bf16[144,128]{1,0:T(8,128)(2,1)S(1)} %get-tuple-element.31.own), channel_id=1, source_target_pairs={{0,16},{2,18},{4,20},{6,22},{8,24},{10,26},{12,28},{14,30},{16,0},... | collective-permute-start | bytes 110600 | tf_op jit(solution)/shard_map/ppermute | solution.py:20
  22.1 4.0 %collective-permute-start.7 = (bf16[144,128]{1,0:T(8,128)(2,1)S(1)}, bf16[144,128]{1,0:T(8,128)(2,1)S(1)}, u32[]{:S(2)}, u32[]{:S(2)}) collective-permute-start(bf16[144,128]{1,0:T(8,128)(2,1)S(1)} %shard_map.124.own), channel_id=1, source_target_pairs={{0,8},{2,10},{4,12},{6,14},{8,0},{10,2},{12,4},{14,6},{16,24},{18,... | collective-permute-start | bytes 110600 | tf_op jit(solution)/shard_map/ppermute | solution.py:20
  22.3 8.0 %collective-permute-start.5 = (bf16[400,128]{1,0:T(8,128)(2,1)S(1)}, bf16[400,128]{1,0:T(8,128)(2,1)S(1)}, u32[]{:S(2)}, u32[]{:S(2)}) collective-permute-start(bf16[400,128]{1,0:T(8,128)(2,1)S(1)} %get-tuple-element.24.pack.own), channel_id=1, source_target_pairs={{0,1},{1,0},{2,3},{3,2},{4,5},{5,4},{6,7},{7,6},{8,9},{9,8},{10,11... | collective-permute-start | bytes 307208 | tf_op jit(solution)/shard_map/ppermute | solution.py:20
  26.2 4.0 %collective-permute-start.8 = (bf16[144,128]{1,0:T(8,128)(2,1)S(1)}, bf16[144,128]{1,0:T(8,128)(2,1)S(1)}, u32[]{:S(2)}, u32[]{:S(2)}) collective-permute-start(bf16[144,128]{1,0:T(8,128)(2,1)S(1)} %shard_map.125.own), channel_id=1, source_target_pairs={{0,4},{2,6},{4,0},{6,2},{8,12},{10,14},{12,8},{14,10},{16,20},{18,... | collective-permute-start | bytes 110600 | tf_op jit(solution)/shard_map/ppermute | solution.py:20
  30.2 8.0 %collective-permute-start.9 = (f32[136,128]{1,0:T(8,128)S(1)}, f32[136,128]{1,0:T(8,128)S(1)}, u32[]{:S(2)}, u32[]{:S(2)}) collective-permute-start(f32[136,128]{1,0:T(8,128)S(1)} %shard_map.126.own), channel_id=1, source_target_pairs={{0,2},{2,0},{4,6},{6,4},{8,10},{10,8},{12,14},{14,12},{16,18},{18,... | collective-permute-start | bytes 208904 | tf_op jit(solution)/shard_map/ppermute | solution.py:20
  31.1 4.3 %collective-permute-start.10 = (bf16[64,256]{1,0:T(8,128)(2,1)S(1)}, bf16[64,256]{1,0:T(8,128)(2,1)S(1)}, u32[]{:S(2)}, u32[]{:S(2)}) collective-permute-start(bf16[64,256]{1,0:T(8,128)(2,1)S(1)} %get-tuple-element.36), channel_id=1, source_target_pairs={{0,2},{2,0},{4,6},{6,4},{8,10},{10,8},{12,14},{14,12},{16,18},{18,... | collective-permute-start | bytes 98312 | tf_op jit(solution)/shard_map/ppermute | solution.py:20
  31.7 3.9 %collective-permute-start.11 = (bf16[64,256]{1,0:T(8,128)(2,1)S(1)}, bf16[64,256]{1,0:T(8,128)(2,1)S(1)}, u32[]{:S(2)}, u32[]{:S(2)}) collective-permute-start(bf16[64,256]{1,0:T(8,128)(2,1)S(1)} %get-tuple-element.37), channel_id=1, source_target_pairs={{0,4},{2,6},{4,0},{6,2},{8,12},{10,14},{12,8},{14,10},{16,20},{18,... | collective-permute-start | bytes 98312 | tf_op jit(solution)/shard_map/ppermute | solution.py:20
  31.7 3.9 %collective-permute-start.12 = (bf16[64,256]{1,0:T(8,128)(2,1)S(1)}, bf16[64,256]{1,0:T(8,128)(2,1)S(1)}, u32[]{:S(2)}, u32[]{:S(2)}) collective-permute-start(bf16[64,256]{1,0:T(8,128)(2,1)S(1)} %get-tuple-element.38), channel_id=1, source_target_pairs={{0,8},{2,10},{4,12},{6,14},{8,0},{10,2},{12,4},{14,6},{16,24},{18,... | collective-permute-start | bytes 98312 | tf_op jit(solution)/shard_map/ppermute | solution.py:20
  32.8 4.8 %collective-permute-start.13 = (bf16[64,256]{1,0:T(8,128)(2,1)S(1)}, bf16[64,256]{1,0:T(8,128)(2,1)S(1)}, u32[]{:S(2)}, u32[]{:S(2)}) collective-permute-start(bf16[64,256]{1,0:T(8,128)(2,1)S(1)} %get-tuple-element.39), channel_id=1, source_target_pairs={{0,16},{2,18},{4,20},{6,22},{8,24},{10,26},{12,28},{14,30},{16,0},... | collective-permute-start | bytes 98312 | tf_op jit(solution)/shard_map/ppermute | solution.py:20

commit v3 on v2

--- a/solution.py
+++ b/solution.py
@@ -52,19 +52,50 @@
     return lax.div(value, divisor)
 
 
+def prepare_kernel(clusters, *refs):
+    size_far, gout, weight, bias_far, own_far = refs[:5]
+    pack, live, live_row, own = refs[5:9]
+    size, bias, sems = refs[9:]
+    rows = gout.shape[0]
+    feats = weight.shape[0]
+    width = rows // clusters
+    copies = [
+        pltpu.make_async_copy(far, close, sems.at[n])
+        for n, (far, close) in enumerate(
+            (
+                (size_far, size),
+                (bias_far, bias),
+                (own_far, own),
+                (weight, pack.at[pl.ds(rows, feats)]),
+                (gout, pack.at[pl.ds(0, rows)]),
+            )
+        )
+    ]
+    for copy in copies:
+        copy.start()
+    for copy in copies[:2]:
+        copy.wait()
+    pack[pl.ds(rows + feats, 16), :] = thirds(bias[...])
+    node = lax.broadcasted_iota(jnp.int32, (width, live.shape[1]), 0)
+    across = lax.broadcasted_iota(jnp.int32, (live_row.shape[0], width), 1)
+    for c in range(clusters):
+        live[pl.ds(c * width, width), :] = (node < size[c]).astype(F32)
+        live_row[:, pl.ds(c * width, width)] = (across < size[c]).astype(F32)
+    for copy in copies[2:]:
+        copy.wait()
+
+
+def count_kernel(count, out):
+    out[...] = jnp.full_like(out, count[0])
+
+
 def build_kernel(levels, clusters, *refs):
-    tiles, src_far, dst_far, count_far, size_far, gout, weight, bias_far, own_far = refs[:9]
-    hi, lo, pack, live, live_row, own = refs[9:15]
-    acc, held, src, dst, count, size, sems, bias, side = refs[15:]
+    tiles, src_far, dst_far, count_far, hi, lo, acc, held, src, dst, count, sems, side = refs
     slots, width = tiles.shape[0], tiles.shape[1]
-    rows, _ = gout.shape
-    feats = weight.shape[0]
     columns = hi.shape[1]
     scalars = [
         pltpu.make_async_copy(far, close, side.at[n])
-        for n, (far, close) in enumerate(
-            ((src_far, src), (dst_far, dst), (count_far, count), (size_far, size))
-        )
+        for n, (far, close) in enumerate(((src_far, src), (dst_far, dst), (count_far, count)))
     ]
     for copy in scalars:
         copy.start()
@@ -79,22 +110,9 @@
     ]
     for copy in fetches:
         copy.start()
-    sides = (
-        pltpu.make_async_copy(gout, pack.at[pl.ds(0, rows)], side.at[4]),
-        pltpu.make_async_copy(weight, pack.at[pl.ds(rows, feats)], side.at[5]),
-        pltpu.make_async_copy(bias_far, bias, side.at[6]),
-        pltpu.make_async_copy(own_far, own, side.at[7]),
-    )
-    for copy in sides:
-        copy.start()
     acc[...] = jnp.zeros_like(acc)
     for copy in scalars:
         copy.wait()
-    node = lax.broadcasted_iota(jnp.int32, (width, live.shape[1]), 0)
-    across = lax.broadcasted_iota(jnp.int32, (live_row.shape[0], width), 1)
-    for c in range(clusters):
-        live[pl.ds(c * width, width), :] = (node < size[c]).astype(F32)
-        live_row[:, pl.ds(c * width, width)] = (across < size[c]).astype(F32)
     used = count[0, 0]
     me = lax.axis_index("rows")
 
@@ -127,9 +145,6 @@
     high = total.astype(BF16)
     hi[...] = high
     lo[...] = (total - high.astype(F32)).astype(BF16)
-    for copy in sides:
-        copy.wait()
-    pack[pl.ds(rows + feats, 16), :] = thirds(bias[...])
 
 
 def merge_kernel(own, other, live, out):
@@ -188,15 +203,9 @@
     value = value.astype(BF16)
     for level in range(levels + 1):
         at = (slice(None), pl.ds(level * nodes, nodes))
-        outs[level][...] = (dot(value, hi[at]) + dot(value, lo[at])).astype(outs[level].dtype)
+        part = dot(value, hi[at]) + dot(value, lo[at])
+        outs[level][...] = part.astype(outs[level].dtype)
     leave.wait()
-
-
-def finish_kernel(live_row, *refs):
-    total = refs[0][...]
-    for part in refs[1:-1]:
-        total = total + part[...].astype(F32)
-    refs[-1][...] = (total * live_row[0:1, :]).astype(BF16)
 
 
 def add_kernel(own, other, out):
@@ -216,10 +225,15 @@
     return kernel_call(add_kernel, near_out(shape, dtype), [VMEM, VMEM], (own, other))
 
 
-def scale_kernel(scale, own, other, grad_weight, grad_bias):
+def finish_kernel(scale, own, other, live_row, *refs):
+    parts, (grad_weight, grad_bias, grad_features) = refs[:-3], refs[-3:]
     feats = grad_weight.shape[0]
     grad_weight[...] = (own[pl.ds(0, feats), :] + other[pl.ds(0, feats), :]) * scale
     grad_bias[...] = (own[pl.ds(feats, 1), :] + other[pl.ds(feats, 1), :]) * scale
+    total = parts[0][...]
+    for part in parts[1:]:
+        total = total + part[...].astype(F32)
+    grad_features[...] = (total * live_row[0:1, :]).astype(BF16)
 
 
 def local(features, adj_tiles, tile_src, tile_dst, tile_count, cluster_size, weight, bias, grad_out):
@@ -232,28 +246,32 @@
     bias = bias.reshape(1, hidden)
     own = features.T
     other = partner(own, "cols", 0)
-    hi, lo, pack, live, live_row, own = kernel_call(
-        functools.partial(build_kernel, levels, clusters),
+    pack, live, live_row, own = kernel_call(
+        functools.partial(prepare_kernel, clusters),
         (
-            near_out((nodes, columns), BF16),
-            near_out((nodes, columns), BF16),
             near_out((nodes + feats + 16, hidden), BF16),
             near_out((nodes, hidden), F32),
             near_out((8, nodes), F32),
             near_out((half, nodes), BF16),
         ),
-        [HBM] * 9,
-        (adj_tiles, tile_src, tile_dst, tile_count.reshape(1, 1), cluster_size, grad_out, weight, bias, own),
+        [HBM] * 5,
+        (cluster_size, grad_out, weight, bias, own),
+        scratch=[pltpu.SMEM((clusters,), jnp.int32), pltpu.VMEM((1, hidden), F32), pltpu.SemaphoreType.DMA((5,))],
+    )
+    used = kernel_call(count_kernel, near_out((8, hidden), jnp.int32), [SMEM], (tile_count,))
+    hi, lo = kernel_call(
+        functools.partial(build_kernel, levels, clusters),
+        (near_out((nodes, columns), BF16), near_out((nodes, columns), BF16)),
+        [HBM] * 3 + [VMEM],
+        (adj_tiles, tile_src, tile_dst, used),
         scratch=[
             pltpu.VMEM((nodes, columns + width), F32),
             pltpu.VMEM((slots, width, width), BF16),
             pltpu.SMEM((slots,), jnp.int32),
             pltpu.SMEM((slots,), jnp.int32),
-            pltpu.SMEM((1, 1), jnp.int32),
-            pltpu.SMEM((clusters,), jnp.int32),
+            pltpu.SMEM((8, hidden), jnp.int32),
             pltpu.SemaphoreType.DMA((-(-slots // TILE_GROUP),)),
-            pltpu.VMEM((1, hidden), F32),
-            pltpu.SemaphoreType.DMA((8,)),
+            pltpu.SemaphoreType.DMA((3,)),
         ],
     )
     table = kernel_call(merge_kernel, near_out((nodes, feats), BF16), [VMEM, VMEM, VMEM], (own, other, live))
@@ -272,7 +290,7 @@
         [VMEM] * (levels + 5),
         (hi, lo, pack, live, *tables),
     )
-    hidden_out, *parts = kernel_call(
+    hidden_out, stays, *parts = kernel_call(
         functools.partial(spread_kernel, levels),
         [jax.ShapeDtypeStruct((nodes, hidden), BF16), near_out((half, nodes), F32)]
         + [near_out((half, nodes), BF16)] * levels,
@@ -283,24 +301,22 @@
     )
     received = []
     for bit in range(levels):
-        received.append(partner(parts[bit + 1], "rows", bit))
+        received.append(partner(parts[bit], "rows", bit))
     moved = None
-    for turn in range(levels):
+    for turn, bit in enumerate(sum_bits(levels)):
         if turn:
             sums = add(sums, moved, F32 if turn + 1 == levels else BF16)
-        moved = partner(sums, "rows", sum_bits(levels)[turn])
-    grad_features = kernel_call(
-        finish_kernel, jax.ShapeDtypeStruct((half, nodes), BF16), [VMEM] * (levels + 2), (live_row, parts[0], *received)
-    )
+        moved = partner(sums, "rows", bit)
     grad_scale = 1.0 / math.sqrt(nodes * lax.axis_size("rows"))
-    grad_weight, grad_bias = kernel_call(
-        functools.partial(scale_kernel, grad_scale),
+    grad_weight, grad_bias, grad_features = kernel_call(
+        functools.partial(finish_kernel, grad_scale),
         (
             jax.ShapeDtypeStruct((feats, hidden), F32),
             jax.ShapeDtypeStruct((1, hidden), F32),
+            jax.ShapeDtypeStruct((half, nodes), BF16),
         ),
-        [VMEM, VMEM],
-        (sums, moved),
+        [VMEM] * (levels + 4),
+        (sums, moved, live_row, stays, *received),
     )
     return (hidden_out, grad_weight, grad_bias.reshape(hidden), grad_features.T)
 

time: 39.1 us -> 38 us (0.972)
  waiting for transfers between devices: 16 us -> 13.4 us
  starting transfers between devices: 16.3 us -> 17.6 us
    ppermute x14, waiting for transfers between devices: 16 us -> 13.4 us  [partner(): lax.ppermute(shard, axis, [(i, i ^ 1 << bit) for i in range(lax.axis_size...]
    ppermute x14, starting transfers between devices: 16.3 us -> 17.6 us  [partner(): lax.ppermute(shard, axis, [(i, i ^ 1 << bit) for i in range(lax.axis_size...]
    pallas_call x9 -> x10, Pallas kernels: 5.27 us -> 5.45 us  [kernel_call(): pl.pallas_call(kernel, out_shape=out_shape, in_specs=in_specs, out_specs=...]
  transfers between devices with their start and end apart: 14 -> 14, of which waited for: 7 -> 8; matrix products, arithmetic and copies ran while one was open for 0% -> 0% of each run, Pallas kernels for 10% -> 10%
where the time goes in v3:
time: 38 us; the launch traced here: 37.8 us
  starting transfers between devices  17.6 us (46%)
  waiting for transfers between devices  13.4 us (35%)
  Pallas kernels  5.45 us (14%)
  between operations  1.39 us (4%)
    ppermute x14, starting transfers between devices, partner(): lax.ppermute(shard, axis, [(i, i ^ 1 << bit) for i in range(lax.axis_size...  17.6 us
    ppermute x14, waiting for transfers between devices, partner(): lax.ppermute(shard, axis, [(i, i ^ 1 << bit) for i in range(lax.axis_size...  13.4 us
    pallas_call x10, Pallas kernels, kernel_call(): pl.pallas_call(kernel, out_shape=out_shape, in_specs=in_specs, out_specs=...  5.45 us
  transfers between devices with their start and end apart: 14, of which 8 were waited for; matrix products, arithmetic and copies ran while one was open for 0% of the time, Pallas kernels for 10%

profile of v3, /device:TPU:0, one launch (start us, length us, event | category | flops | bytes accessed | tf_op | source)
XLA Modules:
  0.0 37.8 jit_solution(16013087376994444201)
XLA Ops:
  0.6 3.0 %collective-permute-start = (bf16[64,256]{1,0:T(8,128)(2,1)}, bf16[64,256]{1,0:T(8,128)(2,1)S(1)}, u32[]{:S(2)}, u32[]{:S(2)}) collective-permute-start(bf16[64,256]{1,0:T(8,128)(2,1)} %bitcast.4), channel_id=1, source_target_pairs={{0,1},{1,0},{2,3},{3,2},{4,5},{5,4},{6,7},{7,6},{8,9},{9,8},{10,11... | collective-permute-start | bytes 98312 | tf_op jit(solution)/shard_map/ppermute | solution.py:20
  3.7 0.9 %shard_map.122 = (bf16[400,128]{1,0:T(8,128)(2,1)S(1)}, f32[256,128]{1,0:T(8,128)S(1)}, f32[8,256]{1,0:T(8,128)S(1)}, bf16[64,256]{1,0:T(8,128)(2,1)S(1)}) custom-call(s32[2]{0:T(128)} %refs_0_.3, bf16[256,128]{1,0:T(8,128)(2,1)} %refs_1_.3, bf16[128,128]{1,0:T(8,128)(2,1)} %refs_2_.3, f32[1,128]{1,0:T(1,128)} %bitcast.6, bf16[64,256]{1,0:T(8,128)(2,1)} %bitcast.5), custom_call_target="tpu_custom_call" | custom-call | tf_op jit(solution)/shard_map/pallas_call | solution.py:30
  4.6 1.2 %collective-permute-done.other = bf16[64,256]{1,0:T(8,128)(2,1)S(1)} collective-permute-done((bf16[64,256]{1,0:T(8,128)(2,1)}, bf16[64,256]{1,0:T(8,128)(2,1)S(1)}, u32[]{:S(2)}, u32[]{:S(2)}) %collective-permute-start) | collective-permute-done | bytes 32800 | tf_op jit(solution)/shard_map/ppermute | solution.py:20
  6.0 2.1 %collective-permute-start.2 = (bf16[256,128]{1,0:T(8,128)(2,1)S(1)}, bf16[256,128]{1,0:T(8,128)(2,1)S(1)}, u32[]{:S(2)}, u32[]{:S(2)}) collective-permute-start(bf16[256,128]{1,0:T(8,128)(2,1)S(1)} %shard_map.123.refs_0_), channel_id=1, source_target_pairs={{0,4},{2,6},{4,0},{6,2},{8,12},{10,14},{12,8},{14,10},{16,20},{18,... | collective-permute-start | bytes 196616 | tf_op jit(solution)/shard_map/ppermute | solution.py:20
  8.1 1.6 %collective-permute-start.3 = (bf16[256,128]{1,0:T(8,128)(2,1)S(1)}, bf16[256,128]{1,0:T(8,128)(2,1)S(1)}, u32[]{:S(2)}, u32[]{:S(2)}) collective-permute-start(bf16[256,128]{1,0:T(8,128)(2,1)S(1)} %shard_map.123.refs_0_), channel_id=1, source_target_pairs={{0,8},{2,10},{4,12},{6,14},{8,0},{10,2},{12,4},{14,6},{16,24},{18,... | collective-permute-start | bytes 196616 | tf_op jit(solution)/shard_map/ppermute | solution.py:20
  9.6 2.6 %collective-permute-start.4 = (bf16[256,128]{1,0:T(8,128)(2,1)S(1)}, bf16[256,128]{1,0:T(8,128)(2,1)S(1)}, u32[]{:S(2)}, u32[]{:S(2)}) collective-permute-start(bf16[256,128]{1,0:T(8,128)(2,1)S(1)} %shard_map.123.refs_0_), channel_id=1, source_target_pairs={{0,16},{2,18},{4,20},{6,22},{8,24},{10,26},{12,28},{14,30},{16,0},... | collective-permute-start | bytes 196616 | tf_op jit(solution)/shard_map/ppermute | solution.py:20
  12.9 2.1 %shard_map.121 = (bf16[256,1280]{1,0:T(8,128)(2,1)S(1)}, bf16[256,1280]{1,0:T(8,128)(2,1)S(1)}) custom-call(bf16[96,128,128]{2,1,0:T(8,128)(2,1)} %refs_0_.2, s32[96]{0:T(128)} %refs_1_.2, s32[96]{0:T(128)} %refs_2_.2, s32[8,128]{1,0:T(8,128)S(1)} %shard_map.120.refs_3_), custom_call_target="tpu_custom_call" | custom-call | tf_op jit(solution)/shard_map/pallas_call | solution.py:30
  15.0 0.8 %collective-permute-done.4.refs_4_ = bf16[256,128]{1,0:T(8,128)(2,1)S(1)} collective-permute-done((bf16[256,128]{1,0:T(8,128)(2,1)S(1)}, bf16[256,128]{1,0:T(8,128)(2,1)S(1)}, u32[]{:S(2)}, u32[]{:S(2)}) %collective-permute-start.4) | collective-permute-done | bytes 65568 | tf_op jit(solution)/shard_map/ppermute | solution.py:20
  15.9 0.8 %shard_map.124 = (bf16[144,128]{1,0:T(8,128)(2,1)S(1)}, bf16[256,128]{1,0:T(8,128)(2,1)S(1)}, bf16[256,128]{1,0:T(8,128)(2,1)S(1)}, bf16[256,128]{1,0:T(8,128)(2,1)S(1)}) custom-call(bf16[256,1280]{1,0:T(8,128)(2,1)S(1)} %get-tuple-element.23.hi, bf16[256,1280]{1,0:T(8,128)(2,1)S(1)} %get-tuple-element.24.lo, ...), custom_call_target="tpu_custom_call" | custom-call | tf_op jit(solution)/shard_map/pallas_call | solution.py:30
  16.7 1.6 %collective-permute-start.6 = (bf16[144,128]{1,0:T(8,128)(2,1)S(1)}, bf16[144,128]{1,0:T(8,128)(2,1)S(1)}, u32[]{:S(2)}, u32[]{:S(2)}) collective-permute-start(bf16[144,128]{1,0:T(8,128)(2,1)S(1)} %get-tuple-element.32.own), channel_id=1, source_target_pairs={{0,16},{2,18},{4,20},{6,22},{8,24},{10,26},{12,28},{14,30},{16,0},... | collective-permute-start | bytes 110600 | tf_op jit(solution)/shard_map/ppermute | solution.py:20
  18.2 3.5 %collective-permute-done.6.other = bf16[144,128]{1,0:T(8,128)(2,1)S(1)} collective-permute-done((bf16[144,128]{1,0:T(8,128)(2,1)S(1)}, bf16[144,128]{1,0:T(8,128)(2,1)S(1)}, u32[]{:S(2)}, u32[]{:S(2)}) %collective-permute-start.6) | collective-permute-done | bytes 36896 | tf_op jit(solution)/shard_map/ppermute | solution.py:20
  21.8 0.2 collective-permute-start.7
  22.1 1.5 %collective-permute-start.5 = (bf16[400,128]{1,0:T(8,128)(2,1)S(1)}, bf16[400,128]{1,0:T(8,128)(2,1)S(1)}, u32[]{:S(2)}, u32[]{:S(2)}) collective-permute-start(bf16[400,128]{1,0:T(8,128)(2,1)S(1)} %get-tuple-element.25.pack.own), channel_id=1, source_target_pairs={{0,1},{1,0},{2,3},{3,2},{4,5},{5,4},{6,7},{7,6},{8,9},{9,8},{10,11... | collective-permute-start | bytes 307208 | tf_op jit(solution)/shard_map/ppermute | solution.py:20
  23.6 2.3 %collective-permute-done.7.other = bf16[144,128]{1,0:T(8,128)(2,1)S(1)} collective-permute-done((bf16[144,128]{1,0:T(8,128)(2,1)S(1)}, bf16[144,128]{1,0:T(8,128)(2,1)S(1)}, u32[]{:S(2)}, u32[]{:S(2)}) %collective-permute-start.7) | collective-permute-done | bytes 36896 | tf_op jit(solution)/shard_map/ppermute | solution.py:20
  25.9 0.6 %collective-permute-start.8 = (bf16[144,128]{1,0:T(8,128)(2,1)S(1)}, bf16[144,128]{1,0:T(8,128)(2,1)S(1)}, u32[]{:S(2)}, u32[]{:S(2)}) collective-permute-start(bf16[144,128]{1,0:T(8,128)(2,1)S(1)} %shard_map.127.own), channel_id=1, source_target_pairs={{0,4},{2,6},{4,0},{6,2},{8,12},{10,14},{12,8},{14,10},{16,20},{18,... | collective-permute-start | bytes 110600 | tf_op jit(solution)/shard_map/ppermute | solution.py:20
  26.4 3.5 %collective-permute-done.8.other = bf16[144,128]{1,0:T(8,128)(2,1)S(1)} collective-permute-done((bf16[144,128]{1,0:T(8,128)(2,1)S(1)}, bf16[144,128]{1,0:T(8,128)(2,1)S(1)}, u32[]{:S(2)}, u32[]{:S(2)}) %collective-permute-start.8) | collective-permute-done | bytes 36896 | tf_op jit(solution)/shard_map/ppermute | solution.py:20
  30.0 0.8 %shard_map.125 = (bf16[256,128]{1,0:T(8,128)(2,1)}, f32[64,256]{1,0:T(8,128)S(1)}, bf16[64,256]{1,0:T(8,128)(2,1)S(1)}, bf16[64,256]{1,0:T(8,128)(2,1)S(1)}, bf1...) custom-call(bf16[256,1280]{1,0:T(8,128)(2,1)S(1)} %get-tuple-element.23.hi, ...), custom_call_target="tpu_custom_call" | custom-call | tf_op jit(solution)/shard_map/pallas_call | solution.py:30
  30.8 0.6 %collective-permute-start.10 = (bf16[64,256]{1,0:T(8,128)(2,1)S(1)}, bf16[64,256]{1,0:T(8,128)(2,1)S(1)}, u32[]{:S(2)}, u32[]{:S(2)}) collective-permute-start(bf16[64,256]{1,0:T(8,128)(2,1)S(1)} %get-tuple-element.35), channel_id=1, source_target_pairs={{0,2},{2,0},{4,6},{6,4},{8,10},{10,8},{12,14},{14,12},{16,18},{18,... | collective-permute-start | bytes 98312 | tf_op jit(solution)/shard_map/ppermute | solution.py:20
  31.4 0.5 %collective-permute-start.11 = (bf16[64,256]{1,0:T(8,128)(2,1)S(1)}, bf16[64,256]{1,0:T(8,128)(2,1)S(1)}, u32[]{:S(2)}, u32[]{:S(2)}) collective-permute-start(bf16[64,256]{1,0:T(8,128)(2,1)S(1)} %get-tuple-element.36), channel_id=1, source_target_pairs={{0,4},{2,6},{4,0},{6,2},{8,12},{10,14},{12,8},{14,10},{16,20},{18,... | collective-permute-start | bytes 98312 | tf_op jit(solution)/shard_map/ppermute | solution.py:20
  32.1 3.0 %collective-permute-start.13 = (bf16[64,256]{1,0:T(8,128)(2,1)S(1)}, bf16[64,256]{1,0:T(8,128)(2,1)S(1)}, u32[]{:S(2)}, u32[]{:S(2)}) collective-permute-start(bf16[64,256]{1,0:T(8,128)(2,1)S(1)} %get-tuple-element.38), channel_id=1, source_target_pairs={{0,16},{2,18},{4,20},{6,22},{8,24},{10,26},{12,28},{14,30},{16,0},... | collective-permute-start | bytes 98312 | tf_op jit(solution)/shard_map/ppermute | solution.py:20
  35.1 0.2 collective-permute-done.11.refs_2_
  35.3 0.8 %collective-permute-done.12.refs_3_ = bf16[64,256]{1,0:T(8,128)(2,1)S(1)} collective-permute-done((bf16[64,256]{1,0:T(8,128)(2,1)S(1)}, bf16[64,256]{1,0:T(8,128)(2,1)S(1)}, u32[]{:S(2)}, u32[]{:S(2)}) %collective-permute-start.12) | collective-permute-done | bytes 32800 | tf_op jit(solution)/shard_map/ppermute | solution.py:20
  36.1 1.0 %collective-permute-done.13.refs_4_ = bf16[64,256]{1,0:T(8,128)(2,1)S(1)} collective-permute-done((bf16[64,256]{1,0:T(8,128)(2,1)S(1)}, bf16[64,256]{1,0:T(8,128)(2,1)S(1)}, u32[]{:S(2)}, u32[]{:S(2)}) %collective-permute-start.13) | collective-permute-done | bytes 32800 | tf_op jit(solution)/shard_map/ppermute | solution.py:20
  37.2 0.7 %shard_map.129 = (f32[128,128]{1,0:T(8,128)}, f32[1,128]{1,0:T(1,128)}, bf16[64,256]{1,0:T(8,128)(2,1)}) custom-call(f32[136,128]{1,0:T(8,128)S(1)} %shard_map.128.own, f32[136,128]{1,0:T(8,128)S(1)} %collective-permute-done.9.other, f32[8,256]{1,0:T(8,128)S(1)} %get-tuple-element.33.live_row, f32[64,256]{1,0:T(8,128)S(1)} %get-tuple-element.34.refs_0_, ...), custom_call_target="tpu_custom_call" | custom-call | tf_op jit(solution)/shard_map/pallas_call | solution.py:30
  (14 shorter events, 0.5 us)
Async XLA Ops:
  0.6 5.1 %collective-permute-start = (bf16[64,256]{1,0:T(8,128)(2,1)}, bf16[64,256]{1,0:T(8,128)(2,1)S(1)}, u32[]{:S(2)}, u32[]{:S(2)}) collective-permute-start(bf16[64,256]{1,0:T(8,128)(2,1)} %bitcast.4), channel_id=1, source_target_pairs={{0,1},{1,0},{2,3},{3,2},{4,5},{5,4},{6,7},{7,6},{8,9},{9,8},{10,11... | collective-permute-start | bytes 98312 | tf_op jit(solution)/shard_map/ppermute | solution.py:20
  5.9 9.1 %collective-permute-start.1 = (bf16[256,128]{1,0:T(8,128)(2,1)S(1)}, bf16[256,128]{1,0:T(8,128)(2,1)S(1)}, u32[]{:S(2)}, u32[]{:S(2)}) collective-permute-start(bf16[256,128]{1,0:T(8,128)(2,1)S(1)} %shard_map.123.refs_0_), channel_id=1, source_target_pairs={{0,2},{2,0},{4,6},{6,4},{8,10},{10,8},{12,14},{14,12},{16,18},{18,... | collective-permute-start | bytes 196616 | tf_op jit(solution)/shard_map/ppermute | solution.py:20
  6.0 9.1 %collective-permute-start.2 = (bf16[256,128]{1,0:T(8,128)(2,1)S(1)}, bf16[256,128]{1,0:T(8,128)(2,1)S(1)}, u32[]{:S(2)}, u32[]{:S(2)}) collective-permute-start(bf16[256,128]{1,0:T(8,128)(2,1)S(1)} %shard_map.123.refs_0_), channel_id=1, source_target_pairs={{0,4},{2,6},{4,0},{6,2},{8,12},{10,14},{12,8},{14,10},{16,20},{18,... | collective-permute-start | bytes 196616 | tf_op jit(solution)/shard_map/ppermute | solution.py:20
  8.1 7.0 %collective-permute-start.3 = (bf16[256,128]{1,0:T(8,128)(2,1)S(1)}, bf16[256,128]{1,0:T(8,128)(2,1)S(1)}, u32[]{:S(2)}, u32[]{:S(2)}) collective-permute-start(bf16[256,128]{1,0:T(8,128)(2,1)S(1)} %shard_map.123.refs_0_), channel_id=1, source_target_pairs={{0,8},{2,10},{4,12},{6,14},{8,0},{10,2},{12,4},{14,6},{16,24},{18,... | collective-permute-start | bytes 196616 | tf_op jit(solution)/shard_map/ppermute | solution.py:20
  9.6 6.2 %collective-permute-start.4 = (bf16[256,128]{1,0:T(8,128)(2,1)S(1)}, bf16[256,128]{1,0:T(8,128)(2,1)S(1)}, u32[]{:S(2)}, u32[]{:S(2)}) collective-permute-start(bf16[256,128]{1,0:T(8,128)(2,1)S(1)} %shard_map.123.refs_0_), channel_id=1, source_target_pairs={{0,16},{2,18},{4,20},{6,22},{8,24},{10,26},{12,28},{14,30},{16,0},... | collective-permute-start | bytes 196616 | tf_op jit(solution)/shard_map/ppermute | solution.py:20
  16.7 5.1 %collective-permute-start.6 = (bf16[144,128]{1,0:T(8,128)(2,1)S(1)}, bf16[144,128]{1,0:T(8,128)(2,1)S(1)}, u32[]{:S(2)}, u32[]{:S(2)}) collective-permute-start(bf16[144,128]{1,0:T(8,128)(2,1)S(1)} %get-tuple-element.32.own), channel_id=1, source_target_pairs={{0,16},{2,18},{4,20},{6,22},{8,24},{10,26},{12,28},{14,30},{16,0},... | collective-permute-start | bytes 110600 | tf_op jit(solution)/shard_map/ppermute | solution.py:20
  21.8 4.0 %collective-permute-start.7 = (bf16[144,128]{1,0:T(8,128)(2,1)S(1)}, bf16[144,128]{1,0:T(8,128)(2,1)S(1)}, u32[]{:S(2)}, u32[]{:S(2)}) collective-permute-start(bf16[144,128]{1,0:T(8,128)(2,1)S(1)} %shard_map.126.own), channel_id=1, source_target_pairs={{0,8},{2,10},{4,12},{6,14},{8,0},{10,2},{12,4},{14,6},{16,24},{18,... | collective-permute-start | bytes 110600 | tf_op jit(solution)/shard_map/ppermute | solution.py:20
  22.1 7.9 %collective-permute-start.5 = (bf16[400,128]{1,0:T(8,128)(2,1)S(1)}, bf16[400,128]{1,0:T(8,128)(2,1)S(1)}, u32[]{:S(2)}, u32[]{:S(2)}) collective-permute-start(bf16[400,128]{1,0:T(8,128)(2,1)S(1)} %get-tuple-element.25.pack.own), channel_id=1, source_target_pairs={{0,1},{1,0},{2,3},{3,2},{4,5},{5,4},{6,7},{7,6},{8,9},{9,8},{10,11... | collective-permute-start | bytes 307208 | tf_op jit(solution)/shard_map/ppermute | solution.py:20
  25.9 4.0 %collective-permute-start.8 = (bf16[144,128]{1,0:T(8,128)(2,1)S(1)}, bf16[144,128]{1,0:T(8,128)(2,1)S(1)}, u32[]{:S(2)}, u32[]{:S(2)}) collective-permute-start(bf16[144,128]{1,0:T(8,128)(2,1)S(1)} %shard_map.127.own), channel_id=1, source_target_pairs={{0,4},{2,6},{4,0},{6,2},{8,12},{10,14},{12,8},{14,10},{16,20},{18,... | collective-permute-start | bytes 110600 | tf_op jit(solution)/shard_map/ppermute | solution.py:20
  29.9 7.3 %collective-permute-start.9 = (f32[136,128]{1,0:T(8,128)S(1)}, f32[136,128]{1,0:T(8,128)S(1)}, u32[]{:S(2)}, u32[]{:S(2)}) collective-permute-start(f32[136,128]{1,0:T(8,128)S(1)} %shard_map.128.own), channel_id=1, source_target_pairs={{0,2},{2,0},{4,6},{6,4},{8,10},{10,8},{12,14},{14,12},{16,18},{18,... | collective-permute-start | bytes 208904 | tf_op jit(solution)/shard_map/ppermute | solution.py:20
  30.8 4.2 %collective-permute-start.10 = (bf16[64,256]{1,0:T(8,128)(2,1)S(1)}, bf16[64,256]{1,0:T(8,128)(2,1)S(1)}, u32[]{:S(2)}, u32[]{:S(2)}) collective-permute-start(bf16[64,256]{1,0:T(8,128)(2,1)S(1)} %get-tuple-element.35), channel_id=1, source_target_pairs={{0,2},{2,0},{4,6},{6,4},{8,10},{10,8},{12,14},{14,12},{16,18},{18,... | collective-permute-start | bytes 98312 | tf_op jit(solution)/shard_map/ppermute | solution.py:20
  31.4 3.9 %collective-permute-start.11 = (bf16[64,256]{1,0:T(8,128)(2,1)S(1)}, bf16[64,256]{1,0:T(8,128)(2,1)S(1)}, u32[]{:S(2)}, u32[]{:S(2)}) collective-permute-start(bf16[64,256]{1,0:T(8,128)(2,1)S(1)} %get-tuple-element.36), channel_id=1, source_target_pairs={{0,4},{2,6},{4,0},{6,2},{8,12},{10,14},{12,8},{14,10},{16,20},{18,... | collective-permute-start | bytes 98312 | tf_op jit(solution)/shard_map/ppermute | solution.py:20
  31.9 4.3 %collective-permute-start.12 = (bf16[64,256]{1,0:T(8,128)(2,1)S(1)}, bf16[64,256]{1,0:T(8,128)(2,1)S(1)}, u32[]{:S(2)}, u32[]{:S(2)}) collective-permute-start(bf16[64,256]{1,0:T(8,128)(2,1)S(1)} %get-tuple-element.37), channel_id=1, source_target_pairs={{0,8},{2,10},{4,12},{6,14},{8,0},{10,2},{12,4},{14,6},{16,24},{18,... | collective-permute-start | bytes 98312 | tf_op jit(solution)/shard_map/ppermute | solution.py:20
  32.1 5.1 %collective-permute-start.13 = (bf16[64,256]{1,0:T(8,128)(2,1)S(1)}, bf16[64,256]{1,0:T(8,128)(2,1)S(1)}, u32[]{:S(2)}, u32[]{:S(2)}) collective-permute-start(bf16[64,256]{1,0:T(8,128)(2,1)S(1)} %get-tuple-element.38), channel_id=1, source_target_pairs={{0,16},{2,18},{4,20},{6,22},{8,24},{10,26},{12,28},{14,30},{16,0},... | collective-permute-start | bytes 98312 | tf_op jit(solution)/shard_map/ppermute | solution.py:20

commit v4 on v3

--- a/solution.py
+++ b/solution.py
@@ -16,8 +16,8 @@
 HBM = pl.BlockSpec(memory_space=pltpu.HBM)
 
 
-def partner(shard, axis, bit):
-    return lax.ppermute(shard, axis, [(i, i ^ 1 << bit) for i in range(lax.axis_size(axis))])
+def partner(shard, axis, mask):
+    return lax.ppermute(shard, axis, [(i, i ^ mask) for i in range(lax.axis_size(axis))])
 
 
 def near(array):
@@ -208,9 +208,12 @@
     leave.wait()
 
 
-def add_kernel(own, other, out):
-    feats = own.shape[0] - 16
-    total = own[...].astype(F32) + other[...].astype(F32)
+def add_kernel(*refs):
+    shares, out = [ref[...].astype(F32) for ref in refs[:-1]], refs[-1]
+    feats = shares[0].shape[0] - 16
+    while len(shares) > 1:
+        shares = [a + b for a, b in zip(shares[::2], shares[1::2])]
+    total = shares[0]
     row = total[feats : feats + 1] + total[feats + 1 : feats + 2] + total[feats + 2 : feats + 3]
     out[pl.ds(0, feats), :] = total[:feats].astype(out.dtype)
     if out.dtype == F32:
@@ -219,10 +222,10 @@
         out[pl.ds(feats, 16), :] = thirds(row)
 
 
-def add(own, other, dtype):
-    rows, columns = own.shape
+def add(shares, dtype):
+    rows, columns = shares[0].shape
     shape = (rows - 8 if dtype == F32 else rows, columns)
-    return kernel_call(add_kernel, near_out(shape, dtype), [VMEM, VMEM], (own, other))
+    return kernel_call(add_kernel, near_out(shape, dtype), [VMEM] * len(shares), shares)
 
 
 def finish_kernel(scale, own, other, live_row, *refs):
@@ -245,7 +248,7 @@
     columns = (levels + 1) * nodes
     bias = bias.reshape(1, hidden)
     own = features.T
-    other = partner(own, "cols", 0)
+    other = partner(own, "cols", 1)
     pack, live, live_row, own = kernel_call(
         functools.partial(prepare_kernel, clusters),
         (
@@ -277,8 +280,8 @@
     table = kernel_call(merge_kernel, near_out((nodes, feats), BF16), [VMEM, VMEM, VMEM], (own, other, live))
     tables = [table]
     for bit in range(levels):
-        tables.append(partner(table, "rows", bit))
-    other_pack = partner(pack, "cols", 0)
+        tables.append(partner(table, "rows", 1 << bit))
+    other_pack = partner(pack, "cols", 1)
     sums, agg, grad_pre, hidden_near = kernel_call(
         functools.partial(main_kernel, levels),
         (
@@ -301,12 +304,15 @@
     )
     received = []
     for bit in range(levels):
-        received.append(partner(parts[bit], "rows", bit))
-    moved = None
-    for turn, bit in enumerate(sum_bits(levels)):
+        received.append(partner(parts[bit], "rows", 1 << bit))
+    turns = sum_turns(levels)
+    moved = []
+    for turn, masks in enumerate(turns):
         if turn:
-            sums = add(sums, moved, F32 if turn + 1 == levels else BF16)
-        moved = partner(sums, "rows", bit)
+            sums = add([sums, *moved], F32 if turn + 1 == len(turns) else BF16)
+        moved = []
+        for mask in masks:
+            moved.append(partner(sums, "rows", mask))
     grad_scale = 1.0 / math.sqrt(nodes * lax.axis_size("rows"))
     grad_weight, grad_bias, grad_features = kernel_call(
         functools.partial(finish_kernel, grad_scale),
@@ -316,13 +322,19 @@
             jax.ShapeDtypeStruct((half, nodes), BF16),
         ),
         [VMEM] * (levels + 4),
-        (sums, moved, live_row, stays, *received),
+        (sums, *moved, live_row, stays, *received),
     )
     return (hidden_out, grad_weight, grad_bias.reshape(hidden), grad_features.T)
 
 
-def sum_bits(levels):
-    return list(reversed(range(levels)))
+def sum_turns(levels):
+    bits = list(reversed(range(1, levels)))
+    turns = []
+    while len(bits) > 1:
+        high, low = 1 << bits.pop(0), 1 << bits.pop(0)
+        turns.append([low, high, low | high])
+    turns += [[1 << bit] for bit in bits]
+    return turns + [[1]]
 
 
 def solution(mesh):

time: 38 us -> 37.8 us (level)
  waiting for transfers between devices: 13.4 us -> 12.1 us
  starting transfers between devices: 17.6 us -> 18.7 us
    ppermute x14 -> x15, waiting for transfers between devices: 13.4 us -> 12.1 us  [partner(): lax.ppermute(shard, axis, [(i, i ^ mask) for i in range(lax.axis_size(axi...]
    ppermute x14 -> x15, starting transfers between devices: 17.6 us -> 18.7 us  [partner(): lax.ppermute(shard, axis, [(i, i ^ mask) for i in range(lax.axis_size(axi...]
    pallas_call x10 -> x9, Pallas kernels: 5.45 us -> 5.44 us  [kernel_call(): pl.pallas_call(kernel, out_shape=out_shape, in_specs=in_specs, out_specs=...]
  transfers between devices with their start and end apart: 14 -> 15, of which waited for: 8 -> 7; matrix products, arithmetic and copies ran while one was open for 0% -> 0% of each run, Pallas kernels for 10% -> 10%
where the time goes in v4:
time: 37.8 us; the launch traced here: 37.7 us
  starting transfers between devices  18.7 us (49%)
  waiting for transfers between devices  12.1 us (32%)
  Pallas kernels  5.44 us (14%)
  between operations  1.39 us (4%)
    ppermute x15, starting transfers between devices, partner(): lax.ppermute(shard, axis, [(i, i ^ mask) for i in range(lax.axis_size(axi...  18.7 us
    ppermute x15, waiting for transfers between devices, partner(): lax.ppermute(shard, axis, [(i, i ^ mask) for i in range(lax.axis_size(axi...  12.1 us
    pallas_call x9, Pallas kernels, kernel_call(): pl.pallas_call(kernel, out_shape=out_shape, in_specs=in_specs, out_specs=...  5.44 us
  transfers between devices with their start and end apart: 15, of which 7 were waited for; matrix products, arithmetic and copies ran while one was open for 0% of the time, Pallas kernels for 10%

profile of v4, /device:TPU:0, one launch (start us, length us, event | category | flops | bytes accessed | tf_op | source)
XLA Modules:
  0.0 37.7 jit_solution(12090749851859682365)
XLA Ops:
  0.6 3.0 %collective-permute-start = (bf16[64,256]{1,0:T(8,128)(2,1)}, bf16[64,256]{1,0:T(8,128)(2,1)S(1)}, u32[]{:S(2)}, u32[]{:S(2)}) collective-permute-start(bf16[64,256]{1,0:T(8,128)(2,1)} %bitcast.4), channel_id=1, source_target_pairs={{0,1},{1,0},{2,3},{3,2},{4,5},{5,4},{6,7},{7,6},{8,9},{9,8},{10,11... | collective-permute-start | bytes 98312 | tf_op jit(solution)/shard_map/ppermute | solution.py:20
  3.7 0.9 %shard_map.122 = (bf16[400,128]{1,0:T(8,128)(2,1)S(1)}, f32[256,128]{1,0:T(8,128)S(1)}, f32[8,256]{1,0:T(8,128)S(1)}, bf16[64,256]{1,0:T(8,128)(2,1)S(1)}) custom-call(s32[2]{0:T(128)} %refs_0_.3, bf16[256,128]{1,0:T(8,128)(2,1)} %refs_1_.3, bf16[128,128]{1,0:T(8,128)(2,1)} %refs_2_.3, f32[1,128]{1,0:T(1,128)} %bitcast.6, bf16[64,256]{1,0:T(8,128)(2,1)} %bitcast.5), custom_call_target="tpu_custom_call" | custom-call | tf_op jit(solution)/shard_map/pallas_call | solution.py:30
  4.6 1.2 %collective-permute-done.other = bf16[64,256]{1,0:T(8,128)(2,1)S(1)} collective-permute-done((bf16[64,256]{1,0:T(8,128)(2,1)}, bf16[64,256]{1,0:T(8,128)(2,1)S(1)}, u32[]{:S(2)}, u32[]{:S(2)}) %collective-permute-start) | collective-permute-done | bytes 32800 | tf_op jit(solution)/shard_map/ppermute | solution.py:20
  6.0 2.1 %collective-permute-start.2 = (bf16[256,128]{1,0:T(8,128)(2,1)S(1)}, bf16[256,128]{1,0:T(8,128)(2,1)S(1)}, u32[]{:S(2)}, u32[]{:S(2)}) collective-permute-start(bf16[256,128]{1,0:T(8,128)(2,1)S(1)} %shard_map.123.refs_0_), channel_id=1, source_target_pairs={{0,4},{2,6},{4,0},{6,2},{8,12},{10,14},{12,8},{14,10},{16,20},{18,... | collective-permute-start | bytes 196616 | tf_op jit(solution)/shard_map/ppermute | solution.py:20
  8.1 1.6 %collective-permute-start.3 = (bf16[256,128]{1,0:T(8,128)(2,1)S(1)}, bf16[256,128]{1,0:T(8,128)(2,1)S(1)}, u32[]{:S(2)}, u32[]{:S(2)}) collective-permute-start(bf16[256,128]{1,0:T(8,128)(2,1)S(1)} %shard_map.123.refs_0_), channel_id=1, source_target_pairs={{0,8},{2,10},{4,12},{6,14},{8,0},{10,2},{12,4},{14,6},{16,24},{18,... | collective-permute-start | bytes 196616 | tf_op jit(solution)/shard_map/ppermute | solution.py:20
  9.6 2.6 %collective-permute-start.4 = (bf16[256,128]{1,0:T(8,128)(2,1)S(1)}, bf16[256,128]{1,0:T(8,128)(2,1)S(1)}, u32[]{:S(2)}, u32[]{:S(2)}) collective-permute-start(bf16[256,128]{1,0:T(8,128)(2,1)S(1)} %shard_map.123.refs_0_), channel_id=1, source_target_pairs={{0,16},{2,18},{4,20},{6,22},{8,24},{10,26},{12,28},{14,30},{16,0},... | collective-permute-start | bytes 196616 | tf_op jit(solution)/shard_map/ppermute | solution.py:20
  12.9 2.1 %shard_map.121 = (bf16[256,1280]{1,0:T(8,128)(2,1)S(1)}, bf16[256,1280]{1,0:T(8,128)(2,1)S(1)}) custom-call(bf16[96,128,128]{2,1,0:T(8,128)(2,1)} %refs_0_.2, s32[96]{0:T(128)} %refs_1_.2, s32[96]{0:T(128)} %refs_2_.2, s32[8,128]{1,0:T(8,128)S(1)} %shard_map.120.refs_3_), custom_call_target="tpu_custom_call" | custom-call | tf_op jit(solution)/shard_map/pallas_call | solution.py:30
  15.0 0.8 %collective-permute-done.4.refs_4_ = bf16[256,128]{1,0:T(8,128)(2,1)S(1)} collective-permute-done((bf16[256,128]{1,0:T(8,128)(2,1)S(1)}, bf16[256,128]{1,0:T(8,128)(2,1)S(1)}, u32[]{:S(2)}, u32[]{:S(2)}) %collective-permute-start.4) | collective-permute-done | bytes 65568 | tf_op jit(solution)/shard_map/ppermute | solution.py:20
  15.9 0.8 %shard_map.124 = (bf16[144,128]{1,0:T(8,128)(2,1)S(1)}, bf16[256,128]{1,0:T(8,128)(2,1)S(1)}, bf16[256,128]{1,0:T(8,128)(2,1)S(1)}, bf16[256,128]{1,0:T(8,128)(2,1)S(1)}) custom-call(bf16[256,1280]{1,0:T(8,128)(2,1)S(1)} %get-tuple-element.23.hi, bf16[256,1280]{1,0:T(8,128)(2,1)S(1)} %get-tuple-element.24.lo, ...), custom_call_target="tpu_custom_call" | custom-call | tf_op jit(solution)/shard_map/pallas_call | solution.py:30
  16.7 0.4 %collective-permute-start.6 = (bf16[144,128]{1,0:T(8,128)(2,1)S(1)}, bf16[144,128]{1,0:T(8,128)(2,1)S(1)}, u32[]{:S(2)}, u32[]{:S(2)}) collective-permute-start(bf16[144,128]{1,0:T(8,128)(2,1)S(1)} %get-tuple-element.32.refs_0_), channel_id=1, source_target_pairs={{0,8},{2,10},{4,12},{6,14},{8,0},{10,2},{12,4},{14,6},{16,24},{18,... | collective-permute-start | bytes 110600 | tf_op jit(solution)/shard_map/ppermute | solution.py:20
  17.1 3.0 %collective-permute-start.7 = (bf16[144,128]{1,0:T(8,128)(2,1)S(1)}, bf16[144,128]{1,0:T(8,128)(2,1)S(1)}, u32[]{:S(2)}, u32[]{:S(2)}) collective-permute-start(bf16[144,128]{1,0:T(8,128)(2,1)S(1)} %get-tuple-element.32.refs_0_), channel_id=1, source_target_pairs={{0,16},{2,18},{4,20},{6,22},{8,24},{10,26},{12,28},{14,30},{16,0},... | collective-permute-start | bytes 110600 | tf_op jit(solution)/shard_map/ppermute | solution.py:20
  20.0 1.1 %collective-permute-start.8 = (bf16[144,128]{1,0:T(8,128)(2,1)S(1)}, bf16[144,128]{1,0:T(8,128)(2,1)S(1)}, u32[]{:S(2)}, u32[]{:S(2)}) collective-permute-start(bf16[144,128]{1,0:T(8,128)(2,1)S(1)} %get-tuple-element.32.refs_0_), channel_id=1, source_target_pairs={{0,24},{2,26},{4,28},{6,30},{8,16},{10,18},{12,20},{14,22},{16,8},... | collective-permute-start | bytes 110600 | tf_op jit(solution)/shard_map/ppermute | solution.py:20
  21.1 1.5 %collective-permute-start.5 = (bf16[400,128]{1,0:T(8,128)(2,1)S(1)}, bf16[400,128]{1,0:T(8,128)(2,1)S(1)}, u32[]{:S(2)}, u32[]{:S(2)}) collective-permute-start(bf16[400,128]{1,0:T(8,128)(2,1)S(1)} %get-tuple-element.25.pack.own), channel_id=1, source_target_pairs={{0,1},{1,0},{2,3},{3,2},{4,5},{5,4},{6,7},{7,6},{8,9},{9,8},{10,11... | collective-permute-start | bytes 307208 | tf_op jit(solution)/shard_map/ppermute | solution.py:20
  22.6 3.2 %collective-permute-done.8.refs_3_ = bf16[144,128]{1,0:T(8,128)(2,1)S(1)} collective-permute-done((bf16[144,128]{1,0:T(8,128)(2,1)S(1)}, bf16[144,128]{1,0:T(8,128)(2,1)S(1)}, u32[]{:S(2)}, u32[]{:S(2)}) %collective-permute-start.8) | collective-permute-done | bytes 36896 | tf_op jit(solution)/shard_map/ppermute | solution.py:20
  25.8 0.6 %collective-permute-start.9 = (bf16[144,128]{1,0:T(8,128)(2,1)S(1)}, bf16[144,128]{1,0:T(8,128)(2,1)S(1)}, u32[]{:S(2)}, u32[]{:S(2)}) collective-permute-start(bf16[144,128]{1,0:T(8,128)(2,1)S(1)} %shard_map.126.refs_0_), channel_id=1, source_target_pairs={{0,4},{2,6},{4,0},{6,2},{8,12},{10,14},{12,8},{14,10},{16,20},{18,... | collective-permute-start | bytes 110600 | tf_op jit(solution)/shard_map/ppermute | solution.py:20
  26.4 3.4 %collective-permute-done.9.refs_1_ = bf16[144,128]{1,0:T(8,128)(2,1)S(1)} collective-permute-done((bf16[144,128]{1,0:T(8,128)(2,1)S(1)}, bf16[144,128]{1,0:T(8,128)(2,1)S(1)}, u32[]{:S(2)}, u32[]{:S(2)}) %collective-permute-start.9) | collective-permute-done | bytes 36896 | tf_op jit(solution)/shard_map/ppermute | solution.py:20
  29.9 0.8 %shard_map.125 = (bf16[256,128]{1,0:T(8,128)(2,1)}, f32[64,256]{1,0:T(8,128)S(1)}, bf16[64,256]{1,0:T(8,128)(2,1)S(1)}, bf16[64,256]{1,0:T(8,128)(2,1)S(1)}, bf1...) custom-call(bf16[256,1280]{1,0:T(8,128)(2,1)S(1)} %get-tuple-element.23.hi, ...), custom_call_target="tpu_custom_call" | custom-call | tf_op jit(solution)/shard_map/pallas_call | solution.py:30
  30.8 0.6 %collective-permute-start.11 = (bf16[64,256]{1,0:T(8,128)(2,1)S(1)}, bf16[64,256]{1,0:T(8,128)(2,1)S(1)}, u32[]{:S(2)}, u32[]{:S(2)}) collective-permute-start(bf16[64,256]{1,0:T(8,128)(2,1)S(1)} %get-tuple-element.35), channel_id=1, source_target_pairs={{0,2},{2,0},{4,6},{6,4},{8,10},{10,8},{12,14},{14,12},{16,18},{18,... | collective-permute-start | bytes 98312 | tf_op jit(solution)/shard_map/ppermute | solution.py:20
  31.3 0.5 %collective-permute-start.12 = (bf16[64,256]{1,0:T(8,128)(2,1)S(1)}, bf16[64,256]{1,0:T(8,128)(2,1)S(1)}, u32[]{:S(2)}, u32[]{:S(2)}) collective-permute-start(bf16[64,256]{1,0:T(8,128)(2,1)S(1)} %get-tuple-element.36), channel_id=1, source_target_pairs={{0,4},{2,6},{4,0},{6,2},{8,12},{10,14},{12,8},{14,10},{16,20},{18,... | collective-permute-start | bytes 98312 | tf_op jit(solution)/shard_map/ppermute | solution.py:20
  31.8 1.6 %collective-permute-start.14 = (bf16[64,256]{1,0:T(8,128)(2,1)S(1)}, bf16[64,256]{1,0:T(8,128)(2,1)S(1)}, u32[]{:S(2)}, u32[]{:S(2)}) collective-permute-start(bf16[64,256]{1,0:T(8,128)(2,1)S(1)} %get-tuple-element.38), channel_id=1, source_target_pairs={{0,16},{2,18},{4,20},{6,22},{8,24},{10,26},{12,28},{14,30},{16,0},... | collective-permute-start | bytes 98312 | tf_op jit(solution)/shard_map/ppermute | solution.py:20
  33.5 1.7 %collective-permute-done.12.refs_2_ = bf16[64,256]{1,0:T(8,128)(2,1)S(1)} collective-permute-done((bf16[64,256]{1,0:T(8,128)(2,1)S(1)}, bf16[64,256]{1,0:T(8,128)(2,1)S(1)}, u32[]{:S(2)}, u32[]{:S(2)}) %collective-permute-start.12) | collective-permute-done | bytes 32800 | tf_op jit(solution)/shard_map/ppermute | solution.py:20
  35.2 0.6 %collective-permute-done.13.refs_3_ = bf16[64,256]{1,0:T(8,128)(2,1)S(1)} collective-permute-done((bf16[64,256]{1,0:T(8,128)(2,1)S(1)}, bf16[64,256]{1,0:T(8,128)(2,1)S(1)}, u32[]{:S(2)}, u32[]{:S(2)}) %collective-permute-start.13) | collective-permute-done | bytes 32800 | tf_op jit(solution)/shard_map/ppermute | solution.py:20
  35.8 1.2 %collective-permute-done.14.refs_4_ = bf16[64,256]{1,0:T(8,128)(2,1)S(1)} collective-permute-done((bf16[64,256]{1,0:T(8,128)(2,1)S(1)}, bf16[64,256]{1,0:T(8,128)(2,1)S(1)}, u32[]{:S(2)}, u32[]{:S(2)}) %collective-permute-start.14) | collective-permute-done | bytes 32800 | tf_op jit(solution)/shard_map/ppermute | solution.py:20
  37.0 0.7 %shard_map.128 = (f32[128,128]{1,0:T(8,128)}, f32[1,128]{1,0:T(1,128)}, bf16[64,256]{1,0:T(8,128)(2,1)}) custom-call(f32[136,128]{1,0:T(8,128)S(1)} %shard_map.127.own, f32[136,128]{1,0:T(8,128)S(1)} %collective-permute-done.10.other, f32[8,256]{1,0:T(8,128)S(1)} %get-tuple-element.33.live_row, f32[64,256]{1,0:T(8,128)S(1)} %get-tuple-element.34.refs_0_, ...), custom_call_target="tpu_custom_call" | custom-call | tf_op jit(solution)/shard_map/pallas_call | solution.py:30
  (15 shorter events, 0.3 us)
Async XLA Ops:
  0.6 5.1 %collective-permute-start = (bf16[64,256]{1,0:T(8,128)(2,1)}, bf16[64,256]{1,0:T(8,128)(2,1)S(1)}, u32[]{:S(2)}, u32[]{:S(2)}) collective-permute-start(bf16[64,256]{1,0:T(8,128)(2,1)} %bitcast.4), channel_id=1, source_target_pairs={{0,1},{1,0},{2,3},{3,2},{4,5},{5,4},{6,7},{7,6},{8,9},{9,8},{10,11... | collective-permute-start | bytes 98312 | tf_op jit(solution)/shard_map/ppermute | solution.py:20
  5.9 9.1 %collective-permute-start.1 = (bf16[256,128]{1,0:T(8,128)(2,1)S(1)}, bf16[256,128]{1,0:T(8,128)(2,1)S(1)}, u32[]{:S(2)}, u32[]{:S(2)}) collective-permute-start(bf16[256,128]{1,0:T(8,128)(2,1)S(1)} %shard_map.123.refs_0_), channel_id=1, source_target_pairs={{0,2},{2,0},{4,6},{6,4},{8,10},{10,8},{12,14},{14,12},{16,18},{18,... | collective-permute-start | bytes 196616 | tf_op jit(solution)/shard_map/ppermute | solution.py:20
  6.0 9.1 %collective-permute-start.2 = (bf16[256,128]{1,0:T(8,128)(2,1)S(1)}, bf16[256,128]{1,0:T(8,128)(2,1)S(1)}, u32[]{:S(2)}, u32[]{:S(2)}) collective-permute-start(bf16[256,128]{1,0:T(8,128)(2,1)S(1)} %shard_map.123.refs_0_), channel_id=1, source_target_pairs={{0,4},{2,6},{4,0},{6,2},{8,12},{10,14},{12,8},{14,10},{16,20},{18,... | collective-permute-start | bytes 196616 | tf_op jit(solution)/shard_map/ppermute | solution.py:20
  8.1 7.0 %collective-permute-start.3 = (bf16[256,128]{1,0:T(8,128)(2,1)S(1)}, bf16[256,128]{1,0:T(8,128)(2,1)S(1)}, u32[]{:S(2)}, u32[]{:S(2)}) collective-permute-start(bf16[256,128]{1,0:T(8,128)(2,1)S(1)} %shard_map.123.refs_0_), channel_id=1, source_target_pairs={{0,8},{2,10},{4,12},{6,14},{8,0},{10,2},{12,4},{14,6},{16,24},{18,... | collective-permute-start | bytes 196616 | tf_op jit(solution)/shard_map/ppermute | solution.py:20
  9.6 6.2 %collective-permute-start.4 = (bf16[256,128]{1,0:T(8,128)(2,1)S(1)}, bf16[256,128]{1,0:T(8,128)(2,1)S(1)}, u32[]{:S(2)}, u32[]{:S(2)}) collective-permute-start(bf16[256,128]{1,0:T(8,128)(2,1)S(1)} %shard_map.123.refs_0_), channel_id=1, source_target_pairs={{0,16},{2,18},{4,20},{6,22},{8,24},{10,26},{12,28},{14,30},{16,0},... | collective-permute-start | bytes 196616 | tf_op jit(solution)/shard_map/ppermute | solution.py:20
  16.7 5.9 %collective-permute-start.6 = (bf16[144,128]{1,0:T(8,128)(2,1)S(1)}, bf16[144,128]{1,0:T(8,128)(2,1)S(1)}, u32[]{:S(2)}, u32[]{:S(2)}) collective-permute-start(bf16[144,128]{1,0:T(8,128)(2,1)S(1)} %get-tuple-element.32.refs_0_), channel_id=1, source_target_pairs={{0,8},{2,10},{4,12},{6,14},{8,0},{10,2},{12,4},{14,6},{16,24},{18,... | collective-permute-start | bytes 110600 | tf_op jit(solution)/shard_map/ppermute | solution.py:20
  17.1 5.5 %collective-permute-start.7 = (bf16[144,128]{1,0:T(8,128)(2,1)S(1)}, bf16[144,128]{1,0:T(8,128)(2,1)S(1)}, u32[]{:S(2)}, u32[]{:S(2)}) collective-permute-start(bf16[144,128]{1,0:T(8,128)(2,1)S(1)} %get-tuple-element.32.refs_0_), channel_id=1, source_target_pairs={{0,16},{2,18},{4,20},{6,22},{8,24},{10,26},{12,28},{14,30},{16,0},... | collective-permute-start | bytes 110600 | tf_op jit(solution)/shard_map/ppermute | solution.py:20
  20.0 5.8 %collective-permute-start.8 = (bf16[144,128]{1,0:T(8,128)(2,1)S(1)}, bf16[144,128]{1,0:T(8,128)(2,1)S(1)}, u32[]{:S(2)}, u32[]{:S(2)}) collective-permute-start(bf16[144,128]{1,0:T(8,128)(2,1)S(1)} %get-tuple-element.32.refs_0_), channel_id=1, source_target_pairs={{0,24},{2,26},{4,28},{6,30},{8,16},{10,18},{12,20},{14,22},{16,8},... | collective-permute-start | bytes 110600 | tf_op jit(solution)/shard_map/ppermute | solution.py:20
  21.1 8.8 %collective-permute-start.5 = (bf16[400,128]{1,0:T(8,128)(2,1)S(1)}, bf16[400,128]{1,0:T(8,128)(2,1)S(1)}, u32[]{:S(2)}, u32[]{:S(2)}) collective-permute-start(bf16[400,128]{1,0:T(8,128)(2,1)S(1)} %get-tuple-element.25.pack.own), channel_id=1, source_target_pairs={{0,1},{1,0},{2,3},{3,2},{4,5},{5,4},{6,7},{7,6},{8,9},{9,8},{10,11... | collective-permute-start | bytes 307208 | tf_op jit(solution)/shard_map/ppermute | solution.py:20
  25.8 4.0 %collective-permute-start.9 = (bf16[144,128]{1,0:T(8,128)(2,1)S(1)}, bf16[144,128]{1,0:T(8,128)(2,1)S(1)}, u32[]{:S(2)}, u32[]{:S(2)}) collective-permute-start(bf16[144,128]{1,0:T(8,128)(2,1)S(1)} %shard_map.126.refs_0_), channel_id=1, source_target_pairs={{0,4},{2,6},{4,0},{6,2},{8,12},{10,14},{12,8},{14,10},{16,20},{18,... | collective-permute-start | bytes 110600 | tf_op jit(solution)/shard_map/ppermute | solution.py:20
  29.8 7.2 %collective-permute-start.10 = (f32[136,128]{1,0:T(8,128)S(1)}, f32[136,128]{1,0:T(8,128)S(1)}, u32[]{:S(2)}, u32[]{:S(2)}) collective-permute-start(f32[136,128]{1,0:T(8,128)S(1)} %shard_map.127.own), channel_id=1, source_target_pairs={{0,2},{2,0},{4,6},{6,4},{8,10},{10,8},{12,14},{14,12},{16,18},{18,... | collective-permute-start | bytes 208904 | tf_op jit(solution)/shard_map/ppermute | solution.py:20
  30.8 2.7 %collective-permute-start.11 = (bf16[64,256]{1,0:T(8,128)(2,1)S(1)}, bf16[64,256]{1,0:T(8,128)(2,1)S(1)}, u32[]{:S(2)}, u32[]{:S(2)}) collective-permute-start(bf16[64,256]{1,0:T(8,128)(2,1)S(1)} %get-tuple-element.35), channel_id=1, source_target_pairs={{0,2},{2,0},{4,6},{6,4},{8,10},{10,8},{12,14},{14,12},{16,18},{18,... | collective-permute-start | bytes 98312 | tf_op jit(solution)/shard_map/ppermute | solution.py:20
  31.3 3.9 %collective-permute-start.12 = (bf16[64,256]{1,0:T(8,128)(2,1)S(1)}, bf16[64,256]{1,0:T(8,128)(2,1)S(1)}, u32[]{:S(2)}, u32[]{:S(2)}) collective-permute-start(bf16[64,256]{1,0:T(8,128)(2,1)S(1)} %get-tuple-element.36), channel_id=1, source_target_pairs={{0,4},{2,6},{4,0},{6,2},{8,12},{10,14},{12,8},{14,10},{16,20},{18,... | collective-permute-start | bytes 98312 | tf_op jit(solution)/shard_map/ppermute | solution.py:20
  31.8 4.0 %collective-permute-start.13 = (bf16[64,256]{1,0:T(8,128)(2,1)S(1)}, bf16[64,256]{1,0:T(8,128)(2,1)S(1)}, u32[]{:S(2)}, u32[]{:S(2)}) collective-permute-start(bf16[64,256]{1,0:T(8,128)(2,1)S(1)} %get-tuple-element.37), channel_id=1, source_target_pairs={{0,8},{2,10},{4,12},{6,14},{8,0},{10,2},{12,4},{14,6},{16,24},{18,... | collective-permute-start | bytes 98312 | tf_op jit(solution)/shard_map/ppermute | solution.py:20
  31.8 5.2 %collective-permute-start.14 = (bf16[64,256]{1,0:T(8,128)(2,1)S(1)}, bf16[64,256]{1,0:T(8,128)(2,1)S(1)}, u32[]{:S(2)}, u32[]{:S(2)}) collective-permute-start(bf16[64,256]{1,0:T(8,128)(2,1)S(1)} %get-tuple-element.38), channel_id=1, source_target_pairs={{0,16},{2,18},{4,20},{6,22},{8,24},{10,26},{12,28},{14,30},{16,0},... | collective-permute-start | bytes 98312 | tf_op jit(solution)/shard_map/ppermute | solution.py:20
